TPU v7x, 256 devices: a whole 4x4x8 slice. The times are simulated.
256 devices in a mesh: grp: 16 (over x, y), seq: 16 (over z, core).
Axes of the slice: x: 4, y: 4, z: 8, core: 2. Of those that a mesh axis runs over, the one named last changes fastest.
Arguments:
- query_input: bfloat16 [32768, 4096], P(('grp', 'seq')), may hold values from -8 to 8
- key_input: bfloat16 [32768, 512], P(('grp', 'seq')), may hold values from -8 to 8
- value_input: bfloat16 [32768, 512], P(('grp', 'seq')), may hold values from -6 to 6
- out_grad: bfloat16 [32768, 4096], P(('grp', 'seq')), may hold values from -6 to 6
- key_blocks: int32 [256, 12], replicated, may hold values from 0 to 255, as said below
- key_counts: int32 [256], replicated, may hold values from 1 to 12, as said below
- block_position: int32 [256], replicated, may hold values from 0 to 255, each once
Outputs:
- attn_out: bfloat16 [32768, 4096], P(('grp', 'seq'))
- query_grad: bfloat16 [32768, 4096], P(('grp', 'seq'))
- key_grad: bfloat16 [32768, 512], P(('grp', 'seq'))
- value_grad: bfloat16 [32768, 512], P(('grp', 'seq'))
Inputs may be any that keep to these rules, and one draw needn't show every extreme that they name: `key_blocks`: in row b the first key_counts[b] entries are distinct, the first is b itself and the others are earlier blocks of the same group of 16 blocks or of the group before; the remaining entries equal b. `key_counts`: the last block's count is 12.
All inputs are finite; a program needn't handle non-finite values.
Results may differ from a plain program's by a relative error of at most 0.015.
Values may be sent and summed in bfloat16 or wider, within the bound.
A program may use at most 128 MiB of HBM per device.

v0:
```python
import math

import jax
import jax.numpy as jnp
from jax import lax
from jax.sharding import PartitionSpec as P

HEADS = 32
KV_HEADS = 4
HEAD_DIM = 128
BLK = 128
KB = 12


def from_behind(array, axis, by):
    length = lax.axis_size(axis)
    pairs = [(i, i + by) for i in range(length) if 0 <= i + by < length]
    return lax.ppermute(array, axis, pairs)


def rope_tables(places):
    offsets = jnp.arange(BLK, dtype=jnp.int32)
    positions = (places[:, None] * BLK + offsets[None, :]).astype(jnp.float32)
    exponents = jnp.arange(HEAD_DIM // 2, dtype=jnp.float32) * (2.0 / HEAD_DIM)
    frequency = jnp.power(jnp.float32(500000.0), -exponents)
    angles = positions[:, :, None] * frequency
    return (jnp.cos(angles), jnp.sin(angles))


def rotate(values, cosine, sine_part):
    half_dim = HEAD_DIM // 2
    first_half = values[..., :half_dim]
    second_half = values[..., half_dim:]
    return jnp.concatenate(
        [
            first_half * cosine - second_half * sine_part,
            second_half * cosine + first_half * sine_part,
        ],
        axis=-1,
    )


def unrotate(values, cosine, sine_part):
    half_dim = HEAD_DIM // 2
    first_half = values[..., :half_dim]
    second_half = values[..., half_dim:]
    return jnp.concatenate(
        [
            first_half * cosine + second_half * sine_part,
            second_half * cosine - first_half * sine_part,
        ],
        axis=-1,
    )


def attend(query_rows, grad_rows, key_store, value_store, listed, usable, diagonal_hit):
    n_blocks = listed.shape[0]
    n_store = key_store.shape[0] // BLK
    group_heads = query_rows.shape[1] // HEAD_DIM
    score_scale = 1.0 / math.sqrt(HEAD_DIM)
    per_step = 1
    for candidate in range(1, n_blocks + 1):
        if n_blocks % candidate == 0 and candidate * BLK * group_heads <= 1024:
            per_step = candidate
    n_steps = n_blocks // per_step
    query_blocks = query_rows.reshape(n_steps, per_step, BLK, group_heads, HEAD_DIM)
    grad_blocks = grad_rows.reshape(n_steps, per_step, BLK, group_heads, HEAD_DIM)
    key_table = key_store.reshape(n_store, BLK, HEAD_DIM)
    value_table = value_store.reshape(n_store, BLK, HEAD_DIM)
    offsets = jnp.arange(BLK, dtype=jnp.int32)
    causal_lower = offsets[None, :] <= offsets[:, None]

    def advance(running, inputs):
        key_acc, value_acc = running
        query_here, grad_here, listed_here, usable_here, diagonal_here = inputs
        key_here = key_table[listed_here]
        value_here = value_table[listed_here]
        allowed = usable_here[:, None, :, None] & (
            jnp.logical_not(diagonal_here)[:, None, :, None] | causal_lower[None, :, None, :]
        )
        scores = (
            jnp.einsum("strd,sjud->srtju", query_here, key_here, preferred_element_type=jnp.float32)
            * score_scale
        )
        scores = jnp.where(allowed[:, None], scores, -jnp.inf)
        row_max = jnp.max(scores, axis=(3, 4), keepdims=True)
        weights = jnp.exp(scores - row_max)
        probs_full = weights / jnp.sum(weights, axis=(3, 4), keepdims=True)
        probs_low = probs_full.astype(jnp.bfloat16)
        attended = lax.optimization_barrier(
            jnp.einsum(
                "srtju,sjud->strd", probs_low, value_here, preferred_element_type=jnp.float32
            ).astype(jnp.bfloat16)
        )
        row_delta = jnp.sum(grad_here.astype(jnp.float32) * attended.astype(jnp.float32), axis=-1)
        dprobs = jnp.einsum(
            "strd,sjud->srtju", grad_here, value_here, preferred_element_type=jnp.float32
        )
        dscores = probs_full * (dprobs - jnp.transpose(row_delta, (0, 2, 1))[:, :, :, None, None])
        dscores_low = dscores.astype(jnp.bfloat16)
        query_part = (
            jnp.einsum(
                "srtju,sjud->strd", dscores_low, key_here, preferred_element_type=jnp.float32
            )
            * score_scale
        ).astype(jnp.bfloat16)
        key_part = (
            jnp.einsum(
                "srtju,strd->sjud", dscores_low, query_here, preferred_element_type=jnp.float32
            )
            * score_scale
        )
        value_part = jnp.einsum(
            "srtju,strd->sjud", probs_low, grad_here, preferred_element_type=jnp.float32
        )
        flat_list = listed_here.reshape(-1)
        key_acc = key_acc.at[flat_list].add(key_part.reshape(-1, BLK, HEAD_DIM))
        value_acc = value_acc.at[flat_list].add(value_part.reshape(-1, BLK, HEAD_DIM))
        return ((key_acc, value_acc), (attended, query_part))

    zero_grads = jnp.zeros((n_store, BLK, HEAD_DIM), jnp.float32)
    inputs = (
        query_blocks,
        grad_blocks,
        listed.reshape(n_steps, per_step, -1),
        usable.reshape(n_steps, per_step, -1),
        diagonal_hit.reshape(n_steps, per_step, -1),
    )
    (key_acc, value_acc), (attended, query_part) = lax.scan(
        advance, (zero_grads, zero_grads), inputs
    )
    out_width = group_heads * HEAD_DIM
    return (
        attended.reshape(n_blocks * BLK, out_width),
        query_part.reshape(n_blocks * BLK, out_width),
        key_acc.reshape(n_store * BLK, HEAD_DIM),
        value_acc.reshape(n_store * BLK, HEAD_DIM),
    )


def local(query_input, key_input, value_input, out_grad, key_blocks, key_counts, block_position):
    n_seq = lax.axis_size("seq")
    group_id = lax.axis_index("grp")
    member_id = lax.axis_index("seq")
    tok_dev = query_input.shape[0]
    blocks_here = tok_dev // BLK
    group_blocks = blocks_here * n_seq
    group_tokens = tok_dev * n_seq
    first_block = (group_id * n_seq + member_id) * blocks_here
    places = lax.dynamic_slice_in_dim(block_position, first_block, blocks_here, 0)
    cosine, sine_part = rope_tables(places)
    cosine = cosine.reshape(tok_dev, 1, HEAD_DIM // 2)
    sine_part = sine_part.reshape(tok_dev, 1, HEAD_DIM // 2)
    q_rot = (
        rotate(query_input.reshape(tok_dev, HEADS, HEAD_DIM).astype(jnp.float32), cosine, sine_part)
        .astype(jnp.bfloat16)
        .reshape(tok_dev, HEADS * HEAD_DIM)
    )
    k_rot = rotate(
        key_input.reshape(tok_dev, KV_HEADS, HEAD_DIM).astype(jnp.float32), cosine, sine_part
    ).astype(jnp.bfloat16)
    kv_pair = jnp.stack([k_rot, value_input.reshape(tok_dev, KV_HEADS, HEAD_DIM)], axis=2)
    share_count = n_seq // KV_HEADS
    spread = jnp.repeat(kv_pair, share_count, axis=1).reshape(tok_dev, n_seq * 2 * HEAD_DIM)
    query_rows, grad_rows, current = (
        lax.all_to_all(q_rot, "seq", split_axis=1, concat_axis=0, tiled=True),
        lax.all_to_all(out_grad, "seq", split_axis=1, concat_axis=0, tiled=True),
        lax.all_to_all(spread, "seq", split_axis=1, concat_axis=0, tiled=True),
    )
    earlier = from_behind(current, "grp", 1)
    query_start = group_id * group_blocks
    listed = lax.dynamic_slice_in_dim(key_blocks, query_start, group_blocks, 0)
    count_rows = lax.dynamic_slice_in_dim(key_counts, query_start, group_blocks, 0)
    query_ids = query_start + jnp.arange(group_blocks, dtype=jnp.int32)
    slot_ids = jnp.arange(KB, dtype=jnp.int32)
    usable = slot_ids[None, :] < count_rows[:, None]
    diagonal_hit = listed == query_ids[:, None]
    local_list = listed - (group_id - 1) * group_blocks
    kv_store = jnp.concatenate([earlier, current], axis=0).reshape(2 * group_tokens, 2, HEAD_DIM)
    attended, dq_rows, key_grads, value_grads = attend(
        query_rows, grad_rows, kv_store[:, 0], kv_store[:, 1], local_list, usable, diagonal_hit
    )
    grad_store = jnp.stack([key_grads, value_grads], axis=1).reshape(2 * group_tokens, 2 * HEAD_DIM)
    earlier_grad = grad_store[:group_tokens]
    current_grad = grad_store[group_tokens:]
    summed = current_grad + from_behind(earlier_grad.astype(jnp.bfloat16), "grp", -1).astype(
        earlier_grad.dtype
    )
    received = lax.all_to_all(summed, "seq", split_axis=0, concat_axis=1, tiled=True)
    own_grad = received.reshape(tok_dev, KV_HEADS, share_count, 2, HEAD_DIM).sum(axis=2)
    out_rows, dq_home = (
        lax.all_to_all(attended, "seq", split_axis=0, concat_axis=1, tiled=True),
        lax.all_to_all(dq_rows, "seq", split_axis=0, concat_axis=1, tiled=True),
    )
    key_grad = (
        unrotate(own_grad[:, :, 0, :], cosine, sine_part)
        .astype(jnp.bfloat16)
        .reshape(tok_dev, KV_HEADS * HEAD_DIM)
    )
    value_grad = own_grad[:, :, 1, :].astype(jnp.bfloat16).reshape(tok_dev, KV_HEADS * HEAD_DIM)
    query_grad = (
        unrotate(dq_home.reshape(tok_dev, HEADS, HEAD_DIM).astype(jnp.float32), cosine, sine_part)
        .astype(jnp.bfloat16)
        .reshape(tok_dev, HEADS * HEAD_DIM)
    )
    return (out_rows, query_grad, key_grad, value_grad)


def solution(mesh):
    in_specs = (
        P(("grp", "seq"), None),
        P(("grp", "seq"), None),
        P(("grp", "seq"), None),
        P(("grp", "seq"), None),
        P(),
        P(),
        P(),
    )
    out_specs = (
        P(("grp", "seq"), None),
        P(("grp", "seq"), None),
        P(("grp", "seq"), None),
        P(("grp", "seq"), None),
    )
    return jax.shard_map(local, mesh=mesh, in_specs=in_specs, out_specs=out_specs, check_vma=False)
```

profile of v0, /device:TPU:1, one launch (start us, length us, event | category | flops | bytes accessed | tf_op | source)
XLA Modules:
  0.0 454.7 jit_solution(790379816822084291)
XLA Ops:
  7.9 10.0 %all-to-all-start = ((bf16[128,16,256]{2,0,1:T(8,128)(2,1)}), bf16[128,16,256]{2,0,1:T(8,128)(2,1)S(1)}, u32[]{:S(2)}, u32[]{:S(2)}) async-start(bf16[128,16,256]{2,0,1:T(8,128)(2,1)} %all_to_all.72), calls=%async_computation | async-start | bytes 2097152 | tf_op jit(solution)/shard_map/all_to_all | solution.py:168
  20.8 25.1 %all-to-all-done = bf16[128,16,256]{2,0,1:T(8,128)(2,1)S(1)} async-done(((bf16[128,16,256]{2,0,1:T(8,128)(2,1)}), bf16[128,16,256]{2,0,1:T(8,128)(2,1)S(1)}, u32[]{:S(2)}, u32[]{:S(2)}) %all-to-all-start) | async-done | bytes 1048608 | tf_op jit(solution)/shard_map/all_to_all | solution.py:168
  45.9 4.2 all-to-all-start.1
  51.5 25.9 %all-to-all-done.1 = bf16[128,16,256]{0,2,1:T(8,128)(2,1)} async-done(((bf16[128,16,256]{0,2,1:T(8,128)(2,1)}), bf16[128,16,256]{0,2,1:T(8,128)(2,1)}, u32[]{:S(2)}, u32[]{:S(2)}) %all-to-all-start.1) | async-done | bytes 1048608 | tf_op jit(solution)/shard_map/all_to_all | solution.py:166
  77.4 4.2 all-to-all-start.2
  81.6 4.2 collective-permute-start
  87.5 20.2 %collective-permute-done = bf16[2048,256]{1,0:T(8,128)(2,1)} collective-permute-done((bf16[2048,256]{1,0:T(8,128)(2,1)S(1)}, bf16[2048,256]{1,0:T(8,128)(2,1)}, u32[]{:S(2)}, u32[]{:S(2)}) %collective-permute-start) | collective-permute-done | bytes 1048608 | tf_op jit(solution)/shard_map/ppermute | solution.py:18
  110.3 2.2 copy.118
  117.1 210.5 %while.17 = (s32[]{:T(128)}, f32[32,128,128]{2,1,0:T(8,128)}, f32[32,128,128]{2,1,0:T(8,128)}, bf16[4,4,128,2,128]{2,4,3,1,0:T(8,128)(2,1)}, bf16[4,4,128,2,128]...) while((s32[]{:T(128)}, f32[32,128,128]{2,1,0:T(8,128)}, ...), condition=%wide.region_6.7_spmd.clone, body=%wide.region_0.6_spmd.clone.sunk | while | flops 2458532352 | bytes 133780712 | solution.py:129
  118.2 2.2 gather_fusion.1
  125.5 3.0 fusion.83
  128.6 10.0 %scatter_fusion.1 = f32[32,128,128]{2,1,0:T(8,128)} fusion(f32[32,128,128]{2,1,0:T(8,128)} %get-tuple-element.308, s32[48]{0:T(128)S(1)} %fusion.78, f32[48,128,128]{2,1,0:T(8,128)S(1)} %bitcast.242), kind=kCustom, calls=%fused_computation.3.clone.clone.1 | custom fusion | flops 786432 | bytes 9437376 | tf_op jit(solution)/shard_map/while/body/eval_jaxpr/scatter-add | solution.py:118
  140.8 5.5 %fusion.81 = bf16[4,128,2,128]{3,1,2,0:T(8,128)(2,1)S(1)} fusion(bf16[4,12,128,128,1]{3,2,4,1,0:T(8,128)(2,1)S(1)} %bitcast.244, f32[4,12,128,128,2]{3,2,4,1,0:T(8,128)} %copy-done.2, f32[4,2,128]{2,1,0:T(2,128)S(1)} %fusion.80, f32[4,2,128]{2,1,0:T(2,128)S(1)} %get-tuple-element.292, pred[4,128,12,128]{1,3,2,0:T(8,128)(4,1)S(1)} %copy-done.4), kind=kOutput, calls=%fused_computation.26.clone.1 | convolution fusion | flops 410648576 | bytes 8921088 | tf_op jit(solution)/shard_map/while/body/eval_jaxpr/srtju,sjud->strd/dot_general | solution.py:91
  146.7 5.6 %fusion.82 = bf16[4,2,128,12,128]{2,4,1,3,0:T(8,128)(2,1)S(1)} fusion(f32[4,2,128]{2,1,0:T(2,128)S(1)} %bitcast.262, bf16[4,12,128,128,1]{3,2,4,1,0:T(8,128)(2,1)} %bitcast.245, bf16[1,4,128,2,128]{2,4,3,1,0:T(8,128)(2,1)} %copy-done.6, f32[4,2,128]{2,1,0:T(2,128)S(1)} %fusion.80, f32[4,2,128]{2,1,0:T(2,128)S(1)} %get-tuple-element.292, ...), kind=kOutput, calls=%fused_computation.7.clone.1 | convolution fusion | flops 413663232 | bytes 12070912 | tf_op jit(solution)/shard_map/while/body/eval_jaxpr/strd,sjud->srtju/dot_general | solution.py:96
  152.3 3.6 bitcast_multiply_fusion.2
  155.9 10.3 %scatter_fusion = f32[32,128,128]{2,1,0:T(8,128)} fusion(f32[32,128,128]{2,1,0:T(8,128)} %get-tuple-element.307, s32[48]{0:T(128)S(1)} %fusion.78, f32[48,128,128]{2,1,0:T(8,128)} %bitcast.238), kind=kCustom, calls=%fused_computation.2.clone.clone.1 | custom fusion | flops 786432 | bytes 9437376 | tf_op jit(solution)/shard_map/while/body/eval_jaxpr/scatter-add | solution.py:117
  166.2 2.9 fusion.84
  171.1 2.2 gather_fusion.1
  178.4 3.0 fusion.83
  181.4 9.7 %scatter_fusion.1 = f32[32,128,128]{2,1,0:T(8,128)} fusion(f32[32,128,128]{2,1,0:T(8,128)} %get-tuple-element.308, s32[48]{0:T(128)S(1)} %fusion.78, f32[48,128,128]{2,1,0:T(8,128)S(1)} %bitcast.242), kind=kCustom, calls=%fused_computation.3.clone.clone.1 | custom fusion | flops 786432 | bytes 9437376 | tf_op jit(solution)/shard_map/while/body/eval_jaxpr/scatter-add | solution.py:118
  193.4 5.5 %fusion.81 = bf16[4,128,2,128]{3,1,2,0:T(8,128)(2,1)S(1)} fusion(bf16[4,12,128,128,1]{3,2,4,1,0:T(8,128)(2,1)S(1)} %bitcast.244, f32[4,12,128,128,2]{3,2,4,1,0:T(8,128)} %copy-done.2, f32[4,2,128]{2,1,0:T(2,128)S(1)} %fusion.80, f32[4,2,128]{2,1,0:T(2,128)S(1)} %get-tuple-element.292, pred[4,128,12,128]{1,3,2,0:T(8,128)(4,1)S(1)} %copy-done.4), kind=kOutput, calls=%fused_computation.26.clone.1 | convolution fusion | flops 410648576 | bytes 8921088 | tf_op jit(solution)/shard_map/while/body/eval_jaxpr/srtju,sjud->strd/dot_general | solution.py:91
  199.3 5.6 %fusion.82 = bf16[4,2,128,12,128]{2,4,1,3,0:T(8,128)(2,1)S(1)} fusion(f32[4,2,128]{2,1,0:T(2,128)S(1)} %bitcast.262, bf16[4,12,128,128,1]{3,2,4,1,0:T(8,128)(2,1)} %bitcast.245, bf16[1,4,128,2,128]{2,4,3,1,0:T(8,128)(2,1)} %copy-done.6, f32[4,2,128]{2,1,0:T(2,128)S(1)} %fusion.80, f32[4,2,128]{2,1,0:T(2,128)S(1)} %get-tuple-element.292, ...), kind=kOutput, calls=%fused_computation.7.clone.1 | convolution fusion | flops 413663232 | bytes 12070912 | tf_op jit(solution)/shard_map/while/body/eval_jaxpr/strd,sjud->srtju/dot_general | solution.py:96
  204.9 3.6 bitcast_multiply_fusion.2
  208.5 10.3 %scatter_fusion = f32[32,128,128]{2,1,0:T(8,128)} fusion(f32[32,128,128]{2,1,0:T(8,128)} %get-tuple-element.307, s32[48]{0:T(128)S(1)} %fusion.78, f32[48,128,128]{2,1,0:T(8,128)} %bitcast.238), kind=kCustom, calls=%fused_computation.2.clone.clone.1 | custom fusion | flops 786432 | bytes 9437376 | tf_op jit(solution)/shard_map/while/body/eval_jaxpr/scatter-add | solution.py:117
  218.8 2.9 fusion.84
  230.9 3.0 fusion.83
  234.0 9.4 %scatter_fusion.1 = f32[32,128,128]{2,1,0:T(8,128)} fusion(f32[32,128,128]{2,1,0:T(8,128)} %get-tuple-element.308, s32[48]{0:T(128)S(1)} %fusion.78, f32[48,128,128]{2,1,0:T(8,128)S(1)} %bitcast.242), kind=kCustom, calls=%fused_computation.3.clone.clone.1 | custom fusion | flops 786432 | bytes 9437376 | tf_op jit(solution)/shard_map/while/body/eval_jaxpr/scatter-add | solution.py:118
  245.6 5.5 %fusion.81 = bf16[4,128,2,128]{3,1,2,0:T(8,128)(2,1)S(1)} fusion(bf16[4,12,128,128,1]{3,2,4,1,0:T(8,128)(2,1)S(1)} %bitcast.244, f32[4,12,128,128,2]{3,2,4,1,0:T(8,128)} %copy-done.2, f32[4,2,128]{2,1,0:T(2,128)S(1)} %fusion.80, f32[4,2,128]{2,1,0:T(2,128)S(1)} %get-tuple-element.292, pred[4,128,12,128]{1,3,2,0:T(8,128)(4,1)S(1)} %copy-done.4), kind=kOutput, calls=%fused_computation.26.clone.1 | convolution fusion | flops 410648576 | bytes 8921088 | tf_op jit(solution)/shard_map/while/body/eval_jaxpr/srtju,sjud->strd/dot_general | solution.py:91
  251.5 5.6 %fusion.82 = bf16[4,2,128,12,128]{2,4,1,3,0:T(8,128)(2,1)S(1)} fusion(f32[4,2,128]{2,1,0:T(2,128)S(1)} %bitcast.262, bf16[4,12,128,128,1]{3,2,4,1,0:T(8,128)(2,1)} %bitcast.245, bf16[1,4,128,2,128]{2,4,3,1,0:T(8,128)(2,1)} %copy-done.6, f32[4,2,128]{2,1,0:T(2,128)S(1)} %fusion.80, f32[4,2,128]{2,1,0:T(2,128)S(1)} %get-tuple-element.292, ...), kind=kOutput, calls=%fused_computation.7.clone.1 | convolution fusion | flops 413663232 | bytes 12070912 | tf_op jit(solution)/shard_map/while/body/eval_jaxpr/strd,sjud->srtju/dot_general | solution.py:96
  257.1 3.6 bitcast_multiply_fusion.2
  260.7 10.6 %scatter_fusion = f32[32,128,128]{2,1,0:T(8,128)} fusion(f32[32,128,128]{2,1,0:T(8,128)} %get-tuple-element.307, s32[48]{0:T(128)S(1)} %fusion.78, f32[48,128,128]{2,1,0:T(8,128)} %bitcast.238), kind=kCustom, calls=%fused_computation.2.clone.clone.1 | custom fusion | flops 786432 | bytes 9437376 | tf_op jit(solution)/shard_map/while/body/eval_jaxpr/scatter-add | solution.py:117
  271.3 2.9 fusion.84
  276.2 2.2 gather_fusion.1
  283.5 3.0 fusion.83
  286.6 9.7 %scatter_fusion.1 = f32[32,128,128]{2,1,0:T(8,128)} fusion(f32[32,128,128]{2,1,0:T(8,128)} %get-tuple-element.308, s32[48]{0:T(128)S(1)} %fusion.78, f32[48,128,128]{2,1,0:T(8,128)S(1)} %bitcast.242), kind=kCustom, calls=%fused_computation.3.clone.clone.1 | custom fusion | flops 786432 | bytes 9437376 | tf_op jit(solution)/shard_map/while/body/eval_jaxpr/scatter-add | solution.py:118
  298.4 5.5 %fusion.81 = bf16[4,128,2,128]{3,1,2,0:T(8,128)(2,1)S(1)} fusion(bf16[4,12,128,128,1]{3,2,4,1,0:T(8,128)(2,1)S(1)} %bitcast.244, f32[4,12,128,128,2]{3,2,4,1,0:T(8,128)} %copy-done.2, f32[4,2,128]{2,1,0:T(2,128)S(1)} %fusion.80, f32[4,2,128]{2,1,0:T(2,128)S(1)} %get-tuple-element.292, pred[4,128,12,128]{1,3,2,0:T(8,128)(4,1)S(1)} %copy-done.4), kind=kOutput, calls=%fused_computation.26.clone.1 | convolution fusion | flops 410648576 | bytes 8921088 | tf_op jit(solution)/shard_map/while/body/eval_jaxpr/srtju,sjud->strd/dot_general | solution.py:91
  304.3 5.6 %fusion.82 = bf16[4,2,128,12,128]{2,4,1,3,0:T(8,128)(2,1)S(1)} fusion(f32[4,2,128]{2,1,0:T(2,128)S(1)} %bitcast.262, bf16[4,12,128,128,1]{3,2,4,1,0:T(8,128)(2,1)} %bitcast.245, bf16[1,4,128,2,128]{2,4,3,1,0:T(8,128)(2,1)} %copy-done.6, f32[4,2,128]{2,1,0:T(2,128)S(1)} %fusion.80, f32[4,2,128]{2,1,0:T(2,128)S(1)} %get-tuple-element.292, ...), kind=kOutput, calls=%fused_computation.7.clone.1 | convolution fusion | flops 413663232 | bytes 12070912 | tf_op jit(solution)/shard_map/while/body/eval_jaxpr/strd,sjud->srtju/dot_general | solution.py:96
  309.9 3.6 bitcast_multiply_fusion.2
  313.5 10.3 %scatter_fusion = f32[32,128,128]{2,1,0:T(8,128)} fusion(f32[32,128,128]{2,1,0:T(8,128)} %get-tuple-element.307, s32[48]{0:T(128)S(1)} %fusion.78, f32[48,128,128]{2,1,0:T(8,128)} %bitcast.238), kind=kCustom, calls=%fused_computation.2.clone.clone.1 | custom fusion | flops 786432 | bytes 9437376 | tf_op jit(solution)/shard_map/while/body/eval_jaxpr/scatter-add | solution.py:117
  323.8 2.9 fusion.84
  327.6 6.7 %all-to-all-start.4 = ((bf16[16,128,256]{1,2,0:T(8,128)(2,1)}), bf16[16,128,256]{1,2,0:T(8,128)(2,1)S(1)}, u32[]{:S(2)}, u32[]{:S(2)}) async-start(bf16[16,128,256]{1,2,0:T(8,128)(2,1)} %bitcast.258), calls=%async_computation.4 | async-start | bytes 2097152 | tf_op jit(solution)/shard_map/all_to_all | solution.py:193
  336.2 2.9 copy.122
  339.1 23.2 %all-to-all-done.4 = bf16[16,128,256]{1,2,0:T(8,128)(2,1)S(1)} async-done(((bf16[16,128,256]{1,2,0:T(8,128)(2,1)}), bf16[16,128,256]{1,2,0:T(8,128)(2,1)S(1)}, u32[]{:S(2)}, u32[]{:S(2)}) %all-to-all-start.4) | async-done | bytes 1048608 | tf_op jit(solution)/shard_map/all_to_all | solution.py:193
  362.3 4.3 all-to-all-start.3
  369.6 25.1 %collective-permute-done.1 = bf16[2048,256]{0,1:T(8,128)(2,1)S(1)} collective-permute-done((bf16[2048,256]{0,1:T(8,128)(2,1)S(1)}, bf16[2048,256]{0,1:T(8,128)(2,1)S(1)}, u32[]{:S(2)}, u32[]{:S(2)}) %collective-permute-start.1) | collective-permute-done | bytes 1048608 | tf_op jit(solution)/shard_map/ppermute | solution.py:18
  396.6 6.8 %all-to-all-start.5 = ((f32[16,128,256]{1,2,0:T(8,128)}), f32[16,128,256]{1,2,0:T(8,128)S(1)}, u32[]{:S(2)}, u32[]{:S(2)}) async-start(f32[16,128,256]{1,2,0:T(8,128)} %copy_bitcast_fusion), calls=%async_computation.5 | async-start | bytes 4194304 | tf_op jit(solution)/shard_map/all_to_all | solution.py:189
  406.0 2.3 copy.102
  408.2 44.3 %all-to-all-done.5 = f32[16,128,256]{1,2,0:T(8,128)S(1)} async-done(((f32[16,128,256]{1,2,0:T(8,128)}), f32[16,128,256]{1,2,0:T(8,128)S(1)}, u32[]{:S(2)}, u32[]{:S(2)}) %all-to-all-start.5) | async-done | bytes 2097184 | tf_op jit(solution)/shard_map/all_to_all | solution.py:189
  (196 shorter events, 71.5 us)
Async XLA Ops:
  5.0 14.4 %copy-start.11 = (f32[128,64]{0,1:T(8,128)}, f32[128,64]{0,1:T(8,128)S(1)}, u32[]{:S(2)}) copy-start(f32[128,64]{0,1:T(8,128)S(1)} %get-tuple-element.206) | copy-start | bytes 98308
  5.0 14.4 %copy-start.13 = (f32[128,64]{0,1:T(8,128)}, f32[128,64]{0,1:T(8,128)S(1)}, u32[]{:S(2)}) copy-start(f32[128,64]{0,1:T(8,128)S(1)} %get-tuple-element.207) | copy-start | bytes 98308
  7.9 38.0 %all-to-all-start = ((bf16[128,16,256]{2,0,1:T(8,128)(2,1)}), bf16[128,16,256]{2,0,1:T(8,128)(2,1)S(1)}, u32[]{:S(2)}, u32[]{:S(2)}) async-start(bf16[128,16,256]{2,0,1:T(8,128)(2,1)} %all_to_all.72), calls=%async_computation | async-start | bytes 2097152 | tf_op jit(solution)/shard_map/all_to_all | solution.py:168
  19.7 30.4 %copy-start.10 = (bf16[128,4096]{1,0:T(8,128)(2,1)S(1)}, bf16[128,4096]{1,0:T(8,128)(2,1)}, u32[]{:S(2)}) copy-start(bf16[128,4096]{1,0:T(8,128)(2,1)} %param.12) | copy-start | bytes 3145732
  45.9 31.5 %all-to-all-start.1 = ((bf16[128,16,256]{0,2,1:T(8,128)(2,1)}), bf16[128,16,256]{0,2,1:T(8,128)(2,1)}, u32[]{:S(2)}, u32[]{:S(2)}) async-start(bf16[128,16,256]{0,2,1:T(8,128)(2,1)} %bitcast.12), calls=%async_computation.1 | async-start | bytes 2097152 | tf_op jit(solution)/shard_map/all_to_all | solution.py:166
  50.1 35.7 %copy-start.15 = (s32[256,12]{0,1:T(8,128)S(1)}, s32[256,12]{0,1:T(8,128)}, u32[]{:S(2)}) copy-start(s32[256,12]{0,1:T(8,128)} %param.13) | copy-start | bytes 36868
  50.2 36.0 %copy-start.16 = (s32[256]{0:T(256)S(1)}, s32[256]{0:T(256)}, u32[]{:S(2)}) copy-start(s32[256]{0:T(256)} %param.14) | copy-start | bytes 3076
  77.4 36.5 %all-to-all-start.2 = ((bf16[128,16,256]{0,2,1:T(8,128)(2,1)}), bf16[128,16,256]{0,2,1:T(8,128)(2,1)}, u32[]{:S(2)}, u32[]{:S(2)}) async-start(bf16[128,16,256]{0,2,1:T(8,128)(2,1)} %bitcast.16), calls=%async_computation.2 | async-start | bytes 2097152 | tf_op jit(solution)/shard_map/all_to_all | solution.py:167
  81.6 26.1 %collective-permute-start = (bf16[2048,256]{1,0:T(8,128)(2,1)S(1)}, bf16[2048,256]{1,0:T(8,128)(2,1)}, u32[]{:S(2)}, u32[]{:S(2)}) collective-permute-start(bf16[2048,256]{1,0:T(8,128)(2,1)S(1)} %bitcast.250), channel_id=1, source_target_pairs={{0,16},{16,32},{32,48},{48,64},{64,80},{80,96},{96,112},{112,128},... | collective-permute-start | bytes 3145736 | tf_op jit(solution)/shard_map/ppermute | solution.py:18
  118.1 4.5 copy-start.3
  120.5 2.1 copy-start.1
  122.6 2.9 copy-start.2
  125.5 3.0 copy-start.6
  138.6 2.2 copy-start.4
  140.7 5.5 %copy-start.5 = (bf16[48,128,128]{2,1,0:T(8,128)(2,1)}, bf16[48,128,128]{2,1,0:T(8,128)(2,1)S(1)}, u32[]{:S(2)}) copy-start(bf16[48,128,128]{2,1,0:T(8,128)(2,1)S(1)} %gather_fusion) | copy-start | bytes 4718596 | tf_op jit(solution)/shard_map/while
  140.8 5.5 %copy-start.7 = (bf16[1,4,128,2,128]{2,4,3,1,0:T(8,128)(2,1)S(1)}, bf16[1,4,128,2,128]{2,4,3,1,0:T(8,128)(2,1)}, u32[]{:S(2)}) copy-start(bf16[1,4,128,2,128]{2,4,3,1,0:T(8,128)(2,1)} %copy-done.6) | copy-start | bytes 786436 | tf_op jit(solution)/shard_map/while
  170.9 4.5 copy-start.3
  173.3 2.1 copy-start.1
  175.5 2.9 copy-start.2
  178.4 3.0 copy-start.6
  191.2 2.2 copy-start.4
  193.3 5.5 %copy-start.5 = (bf16[48,128,128]{2,1,0:T(8,128)(2,1)}, bf16[48,128,128]{2,1,0:T(8,128)(2,1)S(1)}, u32[]{:S(2)}) copy-start(bf16[48,128,128]{2,1,0:T(8,128)(2,1)S(1)} %gather_fusion) | copy-start | bytes 4718596 | tf_op jit(solution)/shard_map/while
  193.3 5.5 %copy-start.7 = (bf16[1,4,128,2,128]{2,4,3,1,0:T(8,128)(2,1)S(1)}, bf16[1,4,128,2,128]{2,4,3,1,0:T(8,128)(2,1)}, u32[]{:S(2)}) copy-start(bf16[1,4,128,2,128]{2,4,3,1,0:T(8,128)(2,1)} %copy-done.6) | copy-start | bytes 786436 | tf_op jit(solution)/shard_map/while
  223.5 4.5 copy-start.3
  225.9 2.1 copy-start.1
  228.0 2.9 copy-start.2
  230.9 3.0 copy-start.6
  243.4 2.2 copy-start.4
  245.6 5.5 %copy-start.5 = (bf16[48,128,128]{2,1,0:T(8,128)(2,1)}, bf16[48,128,128]{2,1,0:T(8,128)(2,1)S(1)}, u32[]{:S(2)}) copy-start(bf16[48,128,128]{2,1,0:T(8,128)(2,1)S(1)} %gather_fusion) | copy-start | bytes 4718596 | tf_op jit(solution)/shard_map/while
  245.6 5.5 %copy-start.7 = (bf16[1,4,128,2,128]{2,4,3,1,0:T(8,128)(2,1)S(1)}, bf16[1,4,128,2,128]{2,4,3,1,0:T(8,128)(2,1)}, u32[]{:S(2)}) copy-start(bf16[1,4,128,2,128]{2,4,3,1,0:T(8,128)(2,1)} %copy-done.6) | copy-start | bytes 786436 | tf_op jit(solution)/shard_map/while
  276.0 4.5 copy-start.3
  278.4 2.1 copy-start.1
  280.6 2.9 copy-start.2
  283.5 3.0 copy-start.6
  296.2 2.2 copy-start.4
  298.4 5.5 %copy-start.5 = (bf16[48,128,128]{2,1,0:T(8,128)(2,1)}, bf16[48,128,128]{2,1,0:T(8,128)(2,1)S(1)}, u32[]{:S(2)}) copy-start(bf16[48,128,128]{2,1,0:T(8,128)(2,1)S(1)} %gather_fusion) | copy-start | bytes 4718596 | tf_op jit(solution)/shard_map/while
  298.4 5.5 %copy-start.7 = (bf16[1,4,128,2,128]{2,4,3,1,0:T(8,128)(2,1)S(1)}, bf16[1,4,128,2,128]{2,4,3,1,0:T(8,128)(2,1)}, u32[]{:S(2)}) copy-start(bf16[1,4,128,2,128]{2,4,3,1,0:T(8,128)(2,1)} %copy-done.6) | copy-start | bytes 786436 | tf_op jit(solution)/shard_map/while
  327.6 6.7 %copy-start = (f32[32,128,128]{2,1,0:T(8,128)S(1)}, f32[32,128,128]{2,1,0:T(8,128)}, u32[]{:S(2)}) copy-start(f32[32,128,128]{2,1,0:T(8,128)} %get-tuple-element.76) | copy-start | bytes 6291460
  327.6 34.7 %all-to-all-start.4 = ((bf16[16,128,256]{1,2,0:T(8,128)(2,1)}), bf16[16,128,256]{1,2,0:T(8,128)(2,1)S(1)}, u32[]{:S(2)}, u32[]{:S(2)}) async-start(bf16[16,128,256]{1,2,0:T(8,128)(2,1)} %bitcast.258), calls=%async_computation.4 | async-start | bytes 2097152 | tf_op jit(solution)/shard_map/all_to_all | solution.py:193
  339.1 27.5 %copy-start.8 = (f32[4096,1,128]{0,2,1:T(8,128)S(1)}, f32[4096,1,128]{0,2,1:T(8,128)}, u32[]{:S(2)}) copy-start(f32[4096,1,128]{0,2,1:T(8,128)} %copy.121) | copy-start | bytes 6291460
  362.3 34.3 %all-to-all-start.3 = ((bf16[16,128,256]{1,2,0:T(8,128)(2,1)}), bf16[16,128,256]{1,2,0:T(8,128)(2,1)}, u32[]{:S(2)}, u32[]{:S(2)}) async-start(bf16[16,128,256]{1,2,0:T(8,128)(2,1)} %bitcast.257), calls=%async_computation.3 | async-start | bytes 2097152 | tf_op jit(solution)/shard_map/all_to_all | solution.py:192
  366.6 2.8 copy-start.9
  368.1 26.6 %collective-permute-start.1 = (bf16[2048,256]{0,1:T(8,128)(2,1)S(1)}, bf16[2048,256]{0,1:T(8,128)(2,1)S(1)}, u32[]{:S(2)}, u32[]{:S(2)}) collective-permute-start(bf16[2048,256]{0,1:T(8,128)(2,1)S(1)} %bitcast.255), channel_id=1, source_target_pairs={{16,0},{32,16},{48,32},{64,48},{80,64},{96,80},{112,96},{128,112},... | collective-permute-start | bytes 3145736 | tf_op jit(solution)/shard_map/ppermute | solution.py:18
  396.6 55.9 %all-to-all-start.5 = ((f32[16,128,256]{1,2,0:T(8,128)}), f32[16,128,256]{1,2,0:T(8,128)S(1)}, u32[]{:S(2)}, u32[]{:S(2)}) async-start(f32[16,128,256]{1,2,0:T(8,128)} %copy_bitcast_fusion), calls=%async_computation.5 | async-start | bytes 4194304 | tf_op jit(solution)/shard_map/all_to_all | solution.py:189
  403.5 0.8 copy-start.12
  403.5 0.8 copy-start.14
where the time goes:
time: 459 us; the launch traced here: 455 us
  waiting for transfers between devices  164 us (36%)
  other arithmetic  98.2 us (21%)
  matrix products  90.5 us (20%)
  local copies, waits for them, and re-layouts  58.1 us (13%)
  starting transfers between devices  41.7 us (9%)
    ppermute x2, waiting for transfers between devices, from_behind(): return lax.ppermute(array, axis, pairs)  45.3 us
    all_to_all x1, waiting for transfers between devices, local(): lax.all_to_all(summed, 'seq', split_axis=0, concat_axis=1, tiled=True)  44.3 us
    scatter-add x4, other arithmetic, advance(): key_acc = key_acc.at[flat_list].add(key_part.reshape(-1, BLK, HEAD_DIM))  41.6 us
    scatter-add x4, other arithmetic, advance(): value_acc.at[flat_list].add(value_part.reshape(-1, BLK, HEAD_DIM))  38.8 us
    all_to_all x1, waiting for transfers between devices, local(): lax.all_to_all(q_rot, 'seq', split_axis=1, concat_axis=0, tiled=True)  25.9 us
    all_to_all x1, waiting for transfers between devices, local(): lax.all_to_all(spread, 'seq', split_axis=1, concat_axis=0, tiled=True)  25.1 us
    all_to_all x1, waiting for transfers between devices, local(): lax.all_to_all(dq_rows, 'seq', split_axis=0, concat_axis=1, tiled=True)  23.2 us
    dot_general x4, matrix products, advance(): jnp.einsum('strd,sjud->srtju', grad_here, value_here, preferred_element_t...  22.4 us
  transfers between devices with their start and end apart: 8, of which 6 were waited for; matrix products, arithmetic and copies ran while one was open for 5% of the time, Pallas kernels for 0%

commit v1 on v0

v1 whole, which is shorter than its diff:
```python
import functools
import math

import jax
import jax.numpy as jnp
from jax import lax
from jax.experimental import pallas as pl
from jax.experimental.pallas import tpu as pltpu
from jax.sharding import PartitionSpec as P

HEADS = 32
KV_HEADS = 4
D = 128
BLK = 128
KB = 12
GB = 16
NK = KB * BLK
HALF = HEADS * D // 2
QW = 8 * D
ROWS = 512
MESH = pl.DeviceIdType.MESH
BF = jnp.bfloat16
F32 = jnp.float32
LOG2E = 1.0 / math.log(2.0)
SCALE = 1.0 / math.sqrt(D)


def nt(a, b):
    return lax.dot_general(a, b, (((1,), (1,)), ((), ())), preferred_element_type=F32)


def nn(a, b):
    return lax.dot_general(a, b, (((1,), (0,)), ((), ())), preferred_element_type=F32)


def kernel(
    n_grp,
    n_z,
    reach,
    kb_ref,
    kc_ref,
    q_ref,
    k_ref,
    v_ref,
    do_ref,
    cos_ref,
    sin_ref,
    out_ref,
    qg_ref,
    kgr_ref,
    vgr_ref,
    kv0,
    kv1,
    pt0,
    pt1,
    rb0,
    rb1,
    sb0,
    sb1,
    ks,
    q_own,
    q_send,
    q_par,
    do_par,
    o_scr,
    dq_scr,
    py_s,
    py_r,
    fo,
    f_s,
    f_r,
    kg,
    vg,
    s_scr,
    e_scr,
    ds_scr,
    q_t,
    do_t,
    inv,
    ss_kv,
    sr_kv,
    ss_x,
    sr_x,
    ss_ag,
    sr_ag,
    ss_ay,
    sr_ay,
    ss_rs,
    sr_rs,
    ss_ry,
    sr_ry,
    ss_f,
    sr_f,
    ss_o,
    sr_o,
):
    kvs, pts, rbs, sbs = (kv0, kv1), (pt0, pt1), (rb0, rb1), (sb0, sb1)
    g = lax.axis_index("grp")
    s_id = lax.axis_index("seq")
    z = s_id // 2
    c = s_id % 2
    other = 1 - c

    def at_z(off):
        return lax.rem(z + off + 2 * n_z, n_z)

    def dev(dg=0, dz=0, flip=False):
        core = other if flip else c
        return {"grp": lax.rem(g + dg + n_grp, n_grp), "seq": at_z(dz) * 2 + core}

    def copy(src, dst, ss, sr, to):
        return pltpu.make_async_remote_copy(
            src_ref=src, dst_ref=dst, send_sem=ss, recv_sem=sr, device_id=to, device_id_type=MESH
        )

    sends = []

    def start(d):
        d.start()
        sends.append(d)

    barrier = pltpu.get_barrier_semaphore()
    peers = [dev(flip=True), dev(dz=1), dev(dz=-1), dev(dg=1), dev(dg=-1)]
    for p in peers:
        pl.semaphore_signal(barrier, inc=1, device_id=p, device_id_type=MESH)

    def cols(base, width=D):
        return pl.ds(pl.multiple_of(base, D), width)

    cos_own, sin_own = cos_ref[1], sin_ref[1]

    def rot(x, cs, sn):
        return x * cs + pltpu.roll(x, D // 2, 1) * sn

    my_slot = GB + 2 * z + c
    for u in range(2):
        for mine in (False, True):
            h = (c if mine else other) * 2 + u
            kr = rot(k_ref[:, cols(h * D)].astype(F32), cos_own, sin_own).astype(BF)
            if mine:
                kvs[u][my_slot, 0] = kr
                kvs[u][my_slot, 1] = v_ref[:, cols(h * D)]
            else:
                ks[u, 0] = kr
                ks[u, 1] = v_ref[:, cols(h * D)]
    pl.semaphore_wait(barrier, len(peers))

    def kv_chip(u):
        return copy(ks.at[u], kvs[u].at[my_slot], ss_kv.at[u], sr_kv.at[u], dev(flip=True))

    def kv_chip_in(u):
        return copy(
            ks.at[u], kvs[u].at[GB + 2 * z + other], ss_kv.at[u], sr_kv.at[u], dev(flip=True)
        )

    def do_copy(u):
        return copy(
            do_ref.at[:, cols(other * HALF + u * QW, QW)],
            do_par.at[:, u * QW : (u + 1) * QW],
            ss_x.at[0, u],
            sr_x.at[0, u],
            dev(flip=True),
        )

    def q_copy(u):
        return copy(
            q_send.at[:, u * QW : (u + 1) * QW],
            q_par.at[:, u * QW : (u + 1) * QW],
            ss_x.at[1, u],
            sr_x.at[1, u],
            dev(flip=True),
        )

    start(kv_chip(0))
    start(kv_chip(1))

    def piece(u, grp, zc, dr, d):
        base = grp * GB + 2 * zc
        if d == n_z // 2:
            return kvs[u].at[pl.ds(base + dr, 1)]
        return kvs[u].at[pl.ds(base, 2)]

    far = n_z // 2

    def ag_out(u, grp, dr, d):
        step = 1 if dr == 0 else -1
        zc = at_z(-step * (d - 1))
        p = piece(u, grp, zc, dr, d)
        return copy(p, p, ss_ag.at[u, grp, dr, d - 1], sr_ag.at[u, grp, dr, d - 1], dev(dz=step))

    def ag_in(u, grp, dr, d):
        step = 1 if dr == 0 else -1
        p = piece(u, grp, at_z(-step * d), dr, d)
        return copy(p, p, ss_ag.at[u, grp, dr, d - 1], sr_ag.at[u, grp, dr, d - 1], dev(dz=step))

    def ay(u, k):
        zc = at_z(k)
        return copy(
            kvs[u].at[pl.ds(GB + 2 * zc, 2)],
            kvs[u].at[pl.ds(2 * zc, 2)],
            ss_ay.at[u, k + 2],
            sr_ay.at[u, k + 2],
            dev(dg=1),
        )

    def ag(u, s):
        if s == 0:
            kv_chip_in(u).wait_recv()
            start(ay(u, 0))
            start(ag_out(u, 1, 0, 1))
            start(ag_out(u, 1, 1, 1))
            return
        k = s - 1
        if k == 0:
            ay(u, 0).wait_recv()
            if reach < 1:
                start(ag_out(u, 0, 0, 1))
                start(ag_out(u, 0, 1, 1))
        else:
            for dr, sign in ((0, -1), (1, 1)):
                if k <= reach:
                    ay(u, sign * k).wait_recv()
                else:
                    ag_in(u, 0, dr, k).wait_recv()
                if k + 1 > reach and k < far:
                    start(ag_out(u, 0, dr, k + 1))
        if s <= far:
            for dr, sign in ((0, -1), (1, 1)):
                ag_in(u, 1, dr, s).wait_recv()
                if s < far:
                    start(ag_out(u, 1, dr, s + 1))
                if s <= reach:
                    start(ay(u, sign * s))

    def q_rope(u):
        for mine in (False, True):
            base = (c if mine else other) * HALF + u * QW
            dst = q_own if mine else q_send
            for h in range(8):
                x = q_ref[:, cols(base + h * D)].astype(F32)
                x = rot(x, cos_own, sin_own) * (SCALE * LOG2E)
                dst[:, u * QW + h * D : u * QW + (h + 1) * D] = x.astype(BF)
            if not mine:
                start(q_copy(u))
                start(do_copy(u))

    row0 = g * GB + 2 * z
    first = (g - 1) * GB
    rows = (row0 + other, row0 + c)

    def invert(kb, carry):
        for b in range(2):
            found = jnp.int32(KB)
            for j in range(KB):
                hit = (kb_ref[rows[b], j] - first == kb) & (j < kc_ref[rows[b]])
                found = jnp.where(hit, j, found)
            inv[b, kb] = found
        return carry

    rr = lax.broadcasted_iota(jnp.int32, (ROWS, BLK), 0) & (BLK - 1)
    cc = lax.broadcasted_iota(jnp.int32, (ROWS, BLK), 1)
    KW = 256

    def gather(u, b):
        for j in range(KB):
            i = jnp.clip(kb_ref[rows[b], j] - first, 0, 2 * GB - 1)
            kg[j * BLK : (j + 1) * BLK, :] = kvs[u][i, 0]
            vg[j * BLK : (j + 1) * BLK, 0:D] = kvs[u][i, 1]

    def compute(u, b, half):
        count = kc_ref[rows[b]]
        r = slice(half * ROWS, (half + 1) * ROWS)
        heads = [half * 4 + x for x in range(4)]
        src_q = q_par if b == 0 else q_own
        q = jnp.concatenate(
            [src_q[:, u * QW + h * D : u * QW + (h + 1) * D] for h in heads], axis=0
        )
        q_t[:, r] = q.T
        mx = None
        for n in range(NK // KW):
            s = nt(q, kg[n * KW : (n + 1) * KW, :])
            for t in range(KW // BLK):
                j = n * (KW // BLK) + t
                st = s[:, t * BLK : (t + 1) * BLK]
                if j == 0:
                    st = jnp.where((cc <= rr) & (j < count), st, -1e30)
                else:
                    st = jnp.where(j < count, st, -1e30)
                s_scr[:, j * BLK : (j + 1) * BLK] = st
                mx = st if mx is None else jnp.maximum(mx, st)
        m = jnp.max(mx, axis=1, keepdims=True)
        for j in range(KB):
            ks_ = slice(j * BLK, (j + 1) * BLK)
            e_scr[r, ks_] = jnp.exp2(s_scr[:, ks_] - m).astype(BF)
        ox = nn(e_scr[r, :], vg[...])
        norm = 1.0 / ox[:, D:]
        o = ox[:, :D] * norm
        if b == 0:
            gr = jnp.concatenate(
                [do_par[:, u * QW + h * D : u * QW + (h + 1) * D] for h in heads], axis=0
            )
        else:
            gr = jnp.concatenate(
                [do_ref[:, cols(c * HALF + u * QW + h * D)] for h in heads], axis=0
            )
        gs = (gr.astype(F32) * norm).astype(BF)
        do_t[:, r] = gs.T
        delta = jnp.sum(gs.astype(F32) * o, axis=1, keepdims=True)
        for n in range(NK // KW):
            ks_ = slice(n * KW, (n + 1) * KW)
            dp = nt(gs, vg[ks_, 0:D])
            ds_scr[r, ks_] = (e_scr[r, ks_].astype(F32) * (dp - delta)).astype(BF)
        dq = nn(ds_scr[r, :], kg[...])
        cs, sn = cos_ref[b] * SCALE, sin_ref[b] * -SCALE
        for x, h in enumerate(heads):
            oh = o[x * BLK : (x + 1) * BLK].astype(BF)
            dh = rot(dq[x * BLK : (x + 1) * BLK], cs, sn).astype(BF)
            if b == 0:
                at = slice(u * QW + h * D, u * QW + (h + 1) * D)
                o_scr[:, at] = oh
                dq_scr[:, at] = dh
            else:
                at = cols(c * HALF + u * QW + h * D)
                out_ref[:, at] = oh
                qg_ref[:, at] = dh

    def o_copy(u, which):
        src, dst = ((o_scr, out_ref), (dq_scr, qg_ref))[which]
        return copy(
            src.at[:, u * QW : (u + 1) * QW],
            dst.at[:, cols(c * HALF + u * QW, QW)],
            ss_o.at[u, which],
            sr_o.at[u, which],
            dev(flip=True),
        )

    def o_copy_in(u, which):
        src, dst = ((o_scr, out_ref), (dq_scr, qg_ref))[which]
        return copy(
            src.at[:, u * QW : (u + 1) * QW],
            dst.at[:, cols(other * HALF + u * QW, QW)],
            ss_o.at[u, which],
            sr_o.at[u, which],
            dev(flip=True),
        )

    def key_grads(u, b):
        if b == 0:
            start(o_copy(u, 0))
            start(o_copy(u, 1))
        for n in range(NK // KW):
            ks_ = slice(n * KW, (n + 1) * KW)
            dv = nn(do_t[...], e_scr[:, ks_])
            dk = nn(q_t[...], ds_scr[:, ks_])
            for t in range(KW // BLK):
                j = n * (KW // BLK) + t
                pts[u][b, j, 0] = dk[:, t * BLK : (t + 1) * BLK].astype(BF)
                pts[u][b, j, 1] = dv[:, t * BLK : (t + 1) * BLK].astype(BF)

    def term(u, slot, w):
        a = pts[u][0, inv[0, slot], w].astype(F32)
        return a + pts[u][1, inv[1, slot], w].astype(F32)

    def rs_out(u, grp, dr, s):
        step = 1 if dr == 0 else -1
        to = dev(dz=step)
        sems = (ss_rs.at[u, grp, dr, s], sr_rs.at[u, grp, dr, s])
        if s == 0:
            return copy(sbs[u].at[grp, dr], rbs[u].at[grp, dr, 0, dr], *sems, to)
        return copy(rbs[u].at[grp, dr, s - 1], rbs[u].at[grp, dr, s], *sems, to)

    def rs(u, s):
        if s == 0:
            for grp in (0, 1):
                for dr in (0, 1):
                    slot = grp * GB + 2 * at_z(far) + dr
                    for w in (0, 1):
                        sbs[u][grp, dr, w] = term(u, slot, w).astype(BF)
                    start(rs_out(u, grp, dr, 0))
        elif s < far:
            for grp in (0, 1):
                for dr in (0, 1):
                    step = 1 if dr == 0 else -1
                    rs_out(u, grp, dr, s - 1).wait_recv()
                    base = grp * GB + 2 * at_z(step * (far - s))
                    for blk in (0, 1):
                        for w in (0, 1):
                            x = term(u, base + blk, w)
                            if s > 1 or blk == dr:
                                x = x + rbs[u][grp, dr, s - 1, blk, w].astype(F32)
                            rbs[u][grp, dr, s - 1, blk, w] = x.astype(BF)
                    start(rs_out(u, grp, dr, s))
        elif s == far:
            for grp in (0, 1):
                for dr in (0, 1):
                    rs_out(u, grp, dr, s - 1).wait_recv()
                base = grp * GB + 2 * z
                for blk in (0, 1):
                    for w in (0, 1):
                        x = term(u, base + blk, w)
                        x = x + rbs[u][grp, 0, far - 1, blk, w].astype(F32)
                        x = x + rbs[u][grp, 1, far - 1, blk, w].astype(F32)
                        if grp == 0:
                            py_s[u, blk, w] = x.astype(BF)
                        else:
                            fo[u, blk, w] = x
                if grp == 0:
                    start(py(u))
        elif s == far + 1:
            py(u).wait_recv()
            for w in (0, 1):
                f_s[u, w] = fo[u, other, w] + py_r[u, other, w].astype(F32)
            start(f_copy(u))
            for w in (0, 1):
                finish(u, c, w, fo[u, c, w] + py_r[u, c, w].astype(F32))
        else:
            f_copy(u).wait_recv()
            for w in (0, 1):
                finish(u, other, w, f_r[u, w])

    def py(u):
        return copy(py_s.at[u], py_r.at[u], ss_ry.at[u], sr_ry.at[u], dev(dg=-1))

    def f_copy(u):
        return copy(f_s.at[u], f_r.at[u], ss_f.at[u], sr_f.at[u], dev(flip=True))

    def finish(u, core, w, x):
        at = cols((core * 2 + u) * D)
        x = x.T
        if w == 0:
            x = rot(x * (1.0 / LOG2E), cos_own, -sin_own)
            kgr_ref[:, at] = x.astype(BF)
        else:
            vgr_ref[:, at] = x.astype(BF)

    def x_wait(u):
        q_copy(u).wait_recv()
        do_copy(u).wait_recv()

    ag(0, 0)
    q_rope(0)
    vg[:, D:] = jnp.ones((NK, D), BF)
    for u in range(2):
        for b in range(2):
            for w in range(2):
                pts[u][b, KB, w] = jnp.zeros((D, BLK), BF)
    lax.fori_loop(0, 2 * GB, invert, 0)
    ag(0, 1)
    q_rope(1)
    ag(0, 2)
    ag(0, 3)
    ag(1, 0)
    ag(0, 4)
    ag(0, 5)
    x_wait(0)
    gather(0, 0)
    compute(0, 0, 0)
    ag(1, 1)
    compute(0, 0, 1)
    key_grads(0, 0)
    ag(1, 2)
    gather(0, 1)
    compute(0, 1, 0)
    ag(1, 3)
    compute(0, 1, 1)
    key_grads(0, 1)
    ag(1, 4)
    rs(0, 0)
    ag(1, 5)
    x_wait(1)
    gather(1, 0)
    compute(1, 0, 0)
    rs(0, 1)
    compute(1, 0, 1)
    key_grads(1, 0)
    rs(0, 2)
    gather(1, 1)
    compute(1, 1, 0)
    rs(0, 3)
    compute(1, 1, 1)
    key_grads(1, 1)
    rs(1, 0)
    rs(0, 4)
    rs(1, 1)
    rs(0, 5)
    rs(1, 2)
    rs(0, 6)
    rs(1, 3)
    rs(1, 4)
    rs(1, 5)
    for u in range(2):
        for which in range(2):
            o_copy_in(u, which).wait_recv()
    rs(1, 6)
    for d in sends:
        d.wait_send()


def local(n_grp, n_seq, q, k, v, do, key_blocks, key_counts, block_position):
    n_z = n_seq // 2
    far = n_z // 2
    me = lax.axis_index("grp") * n_seq + lax.axis_index("seq")
    core = lax.axis_index("seq") % 2
    pair = lax.dynamic_slice_in_dim(block_position, me - core, 2, 0)
    places = jnp.where(core == 0, pair[::-1], pair)
    offsets = jnp.arange(BLK, dtype=jnp.int32)
    positions = (places[:, None] * BLK + offsets[None, :]).astype(F32)
    exponents = jnp.arange(D // 2, dtype=F32) * (2.0 / D)
    frequency = jnp.power(F32(500000.0), -exponents)
    angles = positions[:, :, None] * frequency
    cosine, sine = jnp.cos(angles), jnp.sin(angles)
    cos2 = jnp.concatenate([cosine, cosine], axis=-1)
    sin2 = jnp.concatenate([-sine, sine], axis=-1)
    vm = pl.BlockSpec(memory_space=pltpu.VMEM)
    sm = pl.BlockSpec(memory_space=pltpu.SMEM)
    dma = pltpu.SemaphoreType.DMA
    tok = q.shape[0]
    nslot = 2 * GB
    V = pltpu.VMEM
    scratch = [
        V((nslot, 2, BLK, D), BF),
        V((nslot, 2, BLK, D), BF),
        V((2, KB + 1, 2, D, BLK), BF),
        V((2, KB + 1, 2, D, BLK), BF),
        V((2, 2, far, 2, 2, D, BLK), BF),
        V((2, 2, far, 2, 2, D, BLK), BF),
        V((2, 2, 2, D, BLK), BF),
        V((2, 2, 2, D, BLK), BF),
        V((2, 2, BLK, D), BF),
        V((tok, HALF), BF),
        V((tok, HALF), BF),
        V((tok, HALF), BF),
        V((tok, HALF), BF),
        V((tok, HALF), BF),
        V((tok, HALF), BF),
        V((2, 2, 2, D, BLK), BF),
        V((2, 2, 2, D, BLK), BF),
        V((2, 2, 2, D, BLK), F32),
        V((2, 2, D, BLK), F32),
        V((2, 2, D, BLK), F32),
        V((NK, D), BF),
        V((NK, 2 * D), BF),
        V((ROWS, NK), F32),
        V((8 * BLK, NK), BF),
        V((8 * BLK, NK), BF),
        V((D, 8 * BLK), BF),
        V((D, 8 * BLK), BF),
        pltpu.SMEM((2, nslot), jnp.int32),
    ]
    for shape in (
        (2,),
        (2, 2),
        (2, 2, 2, far),
        (2, 5),
        (2, 2, 2, far),
        (2,),
        (2,),
        (2, 2),
    ):
        scratch += [dma(shape), dma(shape)]
    return pl.pallas_call(
        functools.partial(kernel, n_grp, n_z, 0),
        out_shape=[
            jax.ShapeDtypeStruct(q.shape, BF),
            jax.ShapeDtypeStruct(q.shape, BF),
            jax.ShapeDtypeStruct(k.shape, BF),
            jax.ShapeDtypeStruct(k.shape, BF),
        ],
        in_specs=[sm, sm] + [vm] * 6,
        out_specs=[vm] * 4,
        scratch_shapes=scratch,
        compiler_params=pltpu.CompilerParams(
            collective_id=0, has_side_effects=True, vmem_limit_bytes=60 * 2**20
        ),
    )(key_blocks, key_counts, q, k, v, do, cos2, sin2)


def solution(mesh):
    rows = P(("grp", "seq"), None)
    return jax.shard_map(
        functools.partial(local, mesh.shape["grp"], mesh.shape["seq"]),
        mesh=mesh,
        in_specs=(rows, rows, rows, rows, P(), P(), P()),
        out_specs=(rows, rows, rows, rows),
        check_vma=False,
    )
```

time: 459 us -> 124 us (0.27)
  waiting for transfers between devices: 164 us -> 0 us
  Pallas kernels: 0 us -> 115 us
  other arithmetic: 98.2 us -> 1.54 us
  matrix products: 90.5 us -> 0 us
  local copies, waits for them, and re-layouts: 58.1 us -> 6.63 us
  starting transfers between devices: 41.7 us -> 0 us
    all_to_all x6 -> x0, waiting for transfers between devices: 118 us -> none  [the longest x1 44.3 us: local(): lax.all_to_all(summed, 'seq', split_axis=0, concat_axis=1, tiled=True)]
    pallas_call x0 -> x1, Pallas kernels: none -> 115 us  [local(): pl.pallas_call(functools.partial(kernel, n_grp, n_z, 0), out_shape=[jax.S...]
    dot_general x24 -> x0, matrix products: 90.5 us -> none  [the longest x4 22.4 us: advance(): jnp.einsum('strd,sjud->srtju', grad_here, value_here, preferred_element_t...]
    scatter-add x8 -> x0, other arithmetic: 80.4 us -> none  [the longest x4 41.6 us: advance(): key_acc = key_acc.at[flat_list].add(key_part.reshape(-1, BLK, HEAD_DIM))]
    ppermute x2 -> x0, waiting for transfers between devices: 45.3 us -> none  [from_behind(): return lax.ppermute(array, axis, pairs)]
    all_to_all x6 -> x0, starting transfers between devices: 36.2 us -> none  [the longest x1 9.97 us: local(): lax.all_to_all(spread, 'seq', split_axis=1, concat_axis=0, tiled=True)]
    gather x8 -> x0, local copies, waits for them, and re-layouts: 17.6 us -> none  [the longest x4 8.99 us: advance(): key_here = key_table[listed_here]]
    reduce_sum x9 -> x0, other arithmetic: 7.81 us -> none  [the longest x4 6.76 us: advance(): probs_full = weights / jnp.sum(weights, axis=(3, 4), keepdims=True)]
  transfers between devices with their start and end apart: 8 -> 0, of which waited for: 6 -> 0; matrix products, arithmetic and copies ran while one was open for 5% -> 0% of each run, Pallas kernels for 0% -> 0%
where the time goes in v1:
time: 124 us
  Pallas kernels  115 us (93%)
  local copies, waits for them, and re-layouts  6.63 us (5%)
  other arithmetic  1.54 us (1%)
    pallas_call x1, Pallas kernels, local(): pl.pallas_call(functools.partial(kernel, n_grp, n_z, 0), out_shape=[jax.S...  115 us
    unnamed x15, local copies, waits for them, and re-layouts  6.46 us

profile of v1, /device:TPU:1, one launch (start us, length us, event | category | flops | bytes accessed | tf_op | source)
XLA Modules:
  0.0 124.2 jit_solution(8680305586512891131)
XLA Ops:
  0.6 0.0 copy-start.3
  0.7 0.0 copy-start.4
  0.7 0.7 copy-done.4
  1.3 0.1 dynamic_slice.3
  1.4 0.1 rev.3
  1.5 0.1 fusion.1
  1.6 0.1 add_convert_fusion
  1.7 0.0 copy-done.3
  1.7 0.8 copy.11.kb_ref
  2.5 0.5 fusion
  3.0 0.8 pad_maximum_fusion
  3.8 115.3 %shard_map.102 = (bf16[128,4096]{1,0:T(8,128)(2,1)}, bf16[128,4096]{1,0:T(8,128)(2,1)}, bf16[128,512]{1,0:T(8,128)(2,1)}, bf16[128,512]{1,0:T(8,128)(2,1)}) custom-call(s32[256,12]{1,0:T(8,128)} %copy.11.kb_ref, s32[256]{0:T(256)} %kc_ref.1, bf16[128,4096]{1,0:T(8,128)(2,1)} %q_ref.1, bf16[128,512]{1,0:T(8,128)(2,1)} %k_ref.1, bf16[128,512]{1,0:T(8,128)(2,1)} %v_ref.1, ...), custom_call_target="tpu_custom_call" | custom-call | tf_op jit(solution)/shard_map/pallas_call | solution.py:561
  119.1 0.0 copy-start
  119.2 2.4 %copy.16 = bf16[128,4096]{1,0:T(8,128)(2,1)} copy(bf16[128,4096]{1,0:T(8,128)(2,1)} %get-tuple-element.13) | data formatting | bytes 2097152
  121.5 0.0 copy-done
  121.5 0.0 copy-start.2
  121.5 1.0 copy.17
  122.5 0.1 copy-done.2
  122.6 0.0 copy-start.1
  122.6 0.7 copy.18
  123.2 0.3 copy-done.1
  123.5 0.7 copy.19
  (1 shorter events, 0.0 us)
Async XLA Ops:
  0.6 1.0 copy-start.3
  0.7 0.7 copy-start.4
  119.1 2.4 %copy-start = (bf16[128,4096]{1,0:T(8,128)(2,1)S(1)}, bf16[128,4096]{1,0:T(8,128)(2,1)}, u32[]{:S(2)}) copy-start(bf16[128,4096]{1,0:T(8,128)(2,1)} %get-tuple-element.14) | copy-start | bytes 3145732
  121.5 1.0 copy-start.2
  122.6 1.0 copy-start.1

commit v2 on v0

v2 whole, which is shorter than its diff:
```python
import functools
import math

import jax
import jax.numpy as jnp
import numpy as np
from jax import lax
from jax.experimental import pallas as pl
from jax.experimental.pallas import tpu as pltpu
from jax.sharding import PartitionSpec as P

HEADS = 32
KV_HEADS = 4
D = 128
BLK = 128
KB = 12
GB = 16
NK = KB * BLK
HALF = HEADS * D // 2
QW = 8 * D
KW = 256
ROWS = 512
MESH = pl.DeviceIdType.MESH
BF = jnp.bfloat16
F32 = jnp.float32
LOG2E = 1.0 / math.log(2.0)
SCALE = 1.0 / math.sqrt(D)
PIECES = 30
FREQ = np.tile(500000.0 ** (-np.arange(D // 2) / (D // 2)), 2).astype(np.float32)[None]
FAR = 4
REACH = 2
REACH_R = 2
ORDER = (
    0, 1500000, 1400000, 100, 1600000, 1410000, 1510000, 1000, 300000, 100001, 100011, 300100,
    100101, 100111, 1100, 301000, 101001, 101011, 200001, 100002, 100012, 200011, 100102, 100112,
    200101, 101101, 101111, 200111, 101002, 101012, 301100, 100003, 100013, 201001, 201011,
    100103, 100113, 200002, 101102, 101112, 200012, 101003, 101013, 200102, 10000, 100004, 200112,
    201101, 100114, 200003, 201111, 101113, 101103, 201002, 10100, 200013, 101004, 201012, 110011,
    200103, 201102, 200113, 110001, 201112, 11000, 200004, 101114, 310000, 201003, 110111, 310100,
    110101, 201013, 210011, 11100, 201103, 110012, 210001, 110002, 200114, 901000, 201113, 311000,
    111001, 901100, 201004, 210101, 210111, 110102, 111011, 900000, 110112, 311100, 111101,
    111111, 900100, 210012, 210002, 110003, 110013, 201114, 1001000, 211001, 111002, 1001100,
    210102, 110103, 111012, 1000000, 110113, 211011, 111102, 1000100, 210112, 111112, 1301000,
    210003, 210013, 211101, 1300000, 110004, 501001, 501004, 501011, 501013, 501101, 501103,
    501111, 501114, 401004, 401013, 401103, 401114, 601000, 601100, 211002, 211111, 111003,
    111013, 1101000, 210103, 110114, 211012, 210113, 211102, 111103, 1101100, 210004, 211112,
    111113, 1100000, 501003, 501012, 501102, 501113, 1100100, 401003, 401113, 1201000, 211003,
    211013, 1200000, 210114, 111004, 500001, 500004, 500011, 500013, 500101, 211103, 500103,
    211113, 500111, 500114, 400004, 400013, 400103, 400114, 600000, 401012, 600100, 911000,
    501002, 501112, 401102, 111114, 911100, 211004, 910000, 500003, 500012, 910100, 211114,
    500102, 1011000, 500113, 400003, 1011100, 401101, 400113, 1010000, 401011, 500002, 1010100,
    401002, 1311000, 401112, 1310000, 500112, 400012, 511001, 511004, 511011, 511013, 400102,
    511101, 511103, 511111, 511114, 411004, 411013, 411103, 411114, 611000, 611100, 1111000,
    400002, 401001, 1111100, 401111, 1110000, 400011, 400101, 400112, 511003, 511012, 511113,
    1110100, 511102, 411003, 1211000, 411113, 701100, 400001, 1210000, 701000, 510001, 510004,
    510011, 510013, 510101, 510103, 510111, 510114, 410004, 410013, 410103, 411012, 410114,
    610000, 610100, 400111, 511002, 511112, 411102, 801100, 700000, 801000, 510003, 510012,
    510102, 510113, 410003, 800000, 411011, 411101, 410113, 510002, 700100, 411002, 510112,
    411112, 410012, 410102, 800100, 410002, 411001, 410112, 411111, 410011, 410101, 410001,
    711000, 410111, 711100, 710000, 811000, 710100, 811100, 810000, 810100,
)


def nt(a, b):
    return lax.dot_general(a, b, (((1,), (1,)), ((), ())), preferred_element_type=F32)


def nn(a, b):
    return lax.dot_general(a, b, (((1,), (0,)), ((), ())), preferred_element_type=F32)


def far_of(dr, pb):
    return FAR if dr == pb else FAR - 1


def kernel(n_grp, n_z, reach, reach_r, *refs):
    (
        hbm_in,
        (out_ref, qg_ref, kgr_ref, vgr_ref),
        kvs,
        pts,
        rbs,
        (ks, q_own, q_send, q_par, do_par, o_scr, dq_scr),
        (sb, yb, f_s, f_r),
        (kb_ref, kc_ref, bp_ref, fr_ref, q_ref, k_ref, v_ref, do_ref, cos_ref, sin_ref),
        (kg, vg, s_scr, e_scr, ds_scr, q_t, do_t, g_scr, dl_scr, inv),
        sems,
    ) = split(refs)
    kvs = (kvs[0:2], kvs[2:4])
    pts = (pts[0:2], pts[2:4])
    rbs = (rbs[0:2], rbs[2:4])
    in_sem, ring_sem, ag_sem, rs_sem = sems[:4]
    kv_sem, x_sem, f_sem, o_sem = [sems[4 + 2 * i : 6 + 2 * i] for i in range(4)]
    loads = [
        pltpu.make_async_copy(src, dst, in_sem.at[i])
        for i, (src, dst) in enumerate(
            zip(hbm_in, (kb_ref, kc_ref, bp_ref, fr_ref, q_ref, k_ref, v_ref, do_ref))
        )
    ]
    for i in (2, 3, 5, 6, 4, 7, 0, 1):
        loads[i].start()
    g = lax.axis_index("grp")
    s_id = lax.axis_index("seq")
    z = s_id // 2
    c = s_id % 2
    other = 1 - c
    blk = (c, other)
    steps = (1, -1)

    def at_z(off):
        return lax.rem(z + off + 2 * n_z, n_z)

    def dev(dg=0, dz=0, flip=False):
        core = other if flip else c
        return {"grp": lax.rem(g + dg + n_grp, n_grp), "seq": at_z(dz) * 2 + core}

    sends = []

    def copy(src, dst, sem, at, to):
        return pltpu.make_async_remote_copy(
            src_ref=src,
            dst_ref=dst,
            send_sem=sem[0].at[at],
            recv_sem=sem[1].at[at],
            device_id=to,
            device_id_type=MESH,
        )

    def start(d):
        d.start()
        sends.append(d)

    places = {}

    def ring_copy(src, dst, kind, u, w, key, to):
        at = places.setdefault((kind, u, w), {})
        n = at.setdefault(key, len(at))
        return pltpu.make_async_remote_copy(
            src_ref=src,
            dst_ref=dst,
            send_sem=ring_sem.at[kind, u, w],
            recv_sem=(ag_sem, rs_sem)[kind].at[u, w, n],
            device_id=to,
            device_id_type=MESH,
        )

    barrier = pltpu.get_barrier_semaphore()
    peers = [dev(flip=True), dev(dz=1), dev(dz=-1), dev(dg=1), dev(dg=-1)]
    for p in peers:
        pl.semaphore_signal(barrier, inc=1, device_id=p, device_id_type=MESH)

    def cols(base, width=D):
        return pl.ds(pl.multiple_of(base, D), width)

    def tables(b):
        pos = bp_ref[rows[b]] * BLK + lax.broadcasted_iota(jnp.int32, (BLK, D), 0)
        angle = pos.astype(F32) * fr_ref[...]
        cos_ref[b] = jnp.cos(angle)
        lane = lax.broadcasted_iota(jnp.int32, (BLK, D), 1)
        sin_ref[b] = jnp.where(lane < D // 2, -1.0, 1.0) * jnp.sin(angle)

    row0 = g * GB + 2 * z
    first = (g - 1) * GB
    rows = (row0 + other, row0 + c)
    loads[2].wait()
    loads[3].wait()
    tables(1)
    cos_own, sin_own = cos_ref[1], sin_ref[1]
    loads[5].wait()
    loads[6].wait()

    def rot(x, cs, sn):
        return x * cs + pltpu.roll(x, D // 2, 1) * sn

    def slot(grp, zc, pb):
        return grp * GB + 2 * zc + blk[pb]

    for u in range(2):
        for w in range(2):
            for pb in range(2):
                at = cols((blk[pb] * 2 + u) * D)
                if w == 0:
                    x = rot(k_ref[:, at].astype(F32), cos_own, sin_own).astype(BF)
                else:
                    x = v_ref[:, at]
                if pb == 0:
                    kvs[u][w][slot(1, z, 0)] = x
                else:
                    ks[u, w] = x
    pl.semaphore_wait(barrier, len(peers))

    def kv_chip(u, w, pb):
        return copy(ks.at[u, w], kvs[u][w].at[slot(1, z, pb)], kv_sem, (u, w), dev(flip=True))

    def x_copy(u, which):
        src = q_send.at[:, u * QW : (u + 1) * QW]
        if which == 0:
            src = do_ref.at[:, cols(other * HALF + u * QW, QW)]
        dst = (do_par, q_par)[which].at[:, u * QW : (u + 1) * QW]
        return copy(src, dst, x_sem, (which, u), dev(flip=True))

    def ag_copy(u, w, pb, grp, dr, d, arrived):
        p = kvs[u][w].at[slot(grp, at_z(-steps[dr] * (d if arrived else d - 1)), pb)]
        return ring_copy(p, p, 0, u, w, (pb, grp, dr, d), dev(dz=steps[dr]))

    def ay_copy(u, w, pb, k):
        src = kvs[u][w].at[slot(1, at_z(k), pb)]
        dst = kvs[u][w].at[slot(0, at_z(k), pb)]
        return ring_copy(src, dst, 0, u, w, (pb, k), dev(dg=1))

    def ev_begin(u, w, pb):
        if pb == 1:
            kv_chip(u, w, 1).wait_recv()
        ay_copy(u, w, pb, 0).start()
        for dr in range(2):
            ag_copy(u, w, pb, 1, dr, 1, False).start()

    def ev_own(u, w, pb, dr, k):
        ag_copy(u, w, pb, 1, dr, k, True).wait_recv()
        if k < far_of(dr, pb):
            ag_copy(u, w, pb, 1, dr, k + 1, False).start()
        if k <= reach:
            ay_copy(u, w, pb, -steps[dr] * k).start()

    def ev_prev0(u, w, pb):
        ay_copy(u, w, pb, 0).wait_recv()
        if reach < 1:
            for dr in range(2):
                ag_copy(u, w, pb, 0, dr, 1, False).start()

    def ev_prev(u, w, pb, dr, k):
        if k <= reach:
            ay_copy(u, w, pb, -steps[dr] * k).wait_recv()
        else:
            ag_copy(u, w, pb, 0, dr, k, True).wait_recv()
        if reach < k + 1 <= far_of(dr, pb):
            ag_copy(u, w, pb, 0, dr, k + 1, False).start()

    def q_rope(u):
        if u == 0:
            loads[4].wait()
        for mine in (False, True):
            base = (c if mine else other) * HALF + u * QW
            dst = q_own if mine else q_send
            for h in range(8):
                x = q_ref[:, cols(base + h * D)].astype(F32)
                x = rot(x, cos_own, sin_own) * (SCALE * LOG2E)
                dst[:, u * QW + h * D : u * QW + (h + 1) * D] = x.astype(BF)
            if not mine:
                start(x_copy(u, 1))

    def invert(kb, carry):
        for b in range(2):
            found = jnp.int32(KB)
            for j in range(KB):
                hit = (kb_ref[j, rows[b]] - first == kb) & (j < kc_ref[rows[b]])
                found = jnp.where(hit, j, found)
            inv[b, kb] = found
        return carry

    def setup():
        loads[0].wait()
        loads[1].wait()
        tables(0)
        for b in range(2):
            vg[b, :, D:] = jnp.ones((NK, D), BF)
            for u in range(2):
                for w in range(2):
                    pts[u][w][b, KB] = jnp.zeros((D, BLK), BF)
        lax.fori_loop(0, 2 * GB, invert, 0)

    rr = lax.broadcasted_iota(jnp.int32, (ROWS, BLK), 0) & (BLK - 1)
    cc = lax.broadcasted_iota(jnp.int32, (ROWS, BLK), 1)

    def listed(b, j):
        return jnp.clip(kb_ref[j, rows[b]] - first, 0, 2 * GB - 1)

    def head_rows(half):
        return slice(half * ROWS, (half + 1) * ROWS), [half * 4 + x for x in range(4)]

    def scores(u, b, half):
        if half == 0:
            if b == 0:
                x_copy(u, 1).wait_recv()
            for j in range(KB):
                kg[b, j * BLK : (j + 1) * BLK, :] = kvs[u][0][listed(b, j)]
        count = kc_ref[rows[b]]
        r, heads = head_rows(half)
        src_q = q_par if b == 0 else q_own
        q = jnp.concatenate(
            [src_q[:, u * QW + h * D : u * QW + (h + 1) * D] for h in heads], axis=0
        )
        q_t[b, :, r] = q.T
        mx = None
        for n in range(NK // KW):
            s = nt(q, kg[b, n * KW : (n + 1) * KW, :])
            for t in range(KW // BLK):
                j = n * (KW // BLK) + t
                st = s[:, t * BLK : (t + 1) * BLK]
                if j == 0:
                    st = jnp.where((cc <= rr) & (j < count), st, -1e30)
                else:
                    st = jnp.where(j < count, st, -1e30)
                s_scr[:, j * BLK : (j + 1) * BLK] = st
                mx = st if mx is None else jnp.maximum(mx, st)
        m = jnp.max(mx, axis=1, keepdims=True)
        for j in range(KB):
            ks_ = slice(j * BLK, (j + 1) * BLK)
            e_scr[b, r, ks_] = jnp.exp2(s_scr[:, ks_] - m).astype(BF)

    def attend(u, b, half):
        if half == 0:
            if b == 0:
                x_copy(u, 0).wait_recv()
            for j in range(KB):
                vg[b, j * BLK : (j + 1) * BLK, 0:D] = kvs[u][1][listed(b, j)]
        r, heads = head_rows(half)
        ox = nn(e_scr[b, r, :], vg[b])
        norm = 1.0 / ox[:, D:]
        o = ox[:, :D] * norm
        if b == 0:
            gr = [do_par[:, u * QW + h * D : u * QW + (h + 1) * D] for h in heads]
        else:
            gr = [do_ref[:, cols(c * HALF + u * QW + h * D)] for h in heads]
        gs = (jnp.concatenate(gr, axis=0).astype(F32) * norm).astype(BF)
        do_t[b, :, r] = gs.T
        g_scr[b, r, :] = gs
        delta = jnp.sum(gs.astype(F32) * o, axis=1, keepdims=True)
        dl_scr[b, r, :] = jnp.broadcast_to(delta, (ROWS, D))
        for x, h in enumerate(heads):
            oh = o[x * BLK : (x + 1) * BLK].astype(BF)
            if b == 0:
                o_scr[:, u * QW + h * D : u * QW + (h + 1) * D] = oh
            else:
                out_ref[:, cols(c * HALF + u * QW + h * D)] = oh

    def back(u, b, half):
        r, heads = head_rows(half)
        gs = g_scr[b, r, :]
        delta = dl_scr[b, r, :]
        for n in range(NK // KW):
            dp = nt(gs, vg[b, n * KW : (n + 1) * KW, 0:D])
            for t in range(KW // BLK):
                ks_ = slice(n * KW + t * BLK, n * KW + (t + 1) * BLK)
                x = e_scr[b, r, ks_].astype(F32) * (dp[:, t * BLK : (t + 1) * BLK] - delta)
                ds_scr[b, r, ks_] = x.astype(BF)
        dq = nn(ds_scr[b, r, :], kg[b])
        cs, sn = cos_ref[b] * SCALE, sin_ref[b] * -SCALE
        for x, h in enumerate(heads):
            dh = rot(dq[x * BLK : (x + 1) * BLK], cs, sn).astype(BF)
            if b == 0:
                dq_scr[:, u * QW + h * D : u * QW + (h + 1) * D] = dh
            else:
                qg_ref[:, cols(c * HALF + u * QW + h * D)] = dh

    def o_copy(u, which, core):
        src, dst = ((o_scr, out_ref), (dq_scr, qg_ref))[which]
        return copy(
            src.at[:, u * QW : (u + 1) * QW],
            dst.at[:, cols(core * HALF + u * QW, QW)],
            o_sem,
            (u, which),
            dev(flip=True),
        )

    def grads(w, u, b):
        if b == 0:
            start(o_copy(u, 1 - w, c))
        lhs, rhs = ((q_t, ds_scr), (do_t, e_scr))[w]
        for n in range(NK // KW):
            x = nn(lhs[b], rhs[b, :, n * KW : (n + 1) * KW])
            for t in range(KW // BLK):
                j = n * (KW // BLK) + t
                pts[u][w][b, j] = x[:, t * BLK : (t + 1) * BLK].astype(BF)

    def key_grads(u, b):
        grads(0, u, b)

    def value_grads(u, b):
        grads(1, u, b)

    def do_send(u):
        if u == 0:
            loads[7].wait()
        start(x_copy(u, 0))

    def term(u, w, grp, zc, pb):
        at = slot(grp, zc, pb)
        p = pts[u][w]
        return p[0, inv[0, at]].astype(F32) + p[1, inv[1, at]].astype(F32)

    def rs_copy(u, w, pb, grp, dr, k, arrived=False):
        if k == far_of(dr, pb) and not arrived:
            src = sb.at[u, w, pb, grp, dr]
        else:
            src = rbs[u][w].at[pb, grp, dr, min(k, FAR - 1)]
        dst = rbs[u][w].at[pb, grp, dr, k - 1]
        return ring_copy(src, dst, 1, u, w, (pb, grp, dr, k), dev(dz=steps[dr]))

    def ry_copy(u, w, pb, dr, k):
        at = k if dr == 0 else -k
        src = rbs[u][w].at[pb, 0, dr, k]
        return ring_copy(src, yb.at[u, w, pb, at + 2], 1, u, w, (pb, at), dev(dg=-1))

    def ev_sum_own(u, w, pb, dr, k):
        x = term(u, w, 1, at_z(steps[dr] * k), pb)
        dst = sb.at[u, w, pb, 1, dr]
        if k < far_of(dr, pb):
            rs_copy(u, w, pb, 1, dr, k + 1, True).wait_recv()
            dst = rbs[u][w].at[pb, 1, dr, k]
            x = x + dst[...].astype(F32)
        if k <= reach_r:
            ry_copy(u, w, pb, dr, k).wait_recv()
            x = x + yb[u, w, pb, (k if dr == 0 else -k) + 2].astype(F32)
        dst[...] = x.astype(BF)
        rs_copy(u, w, pb, 1, dr, k).start()

    def ev_sum_prev(u, w, pb, dr, k):
        x = term(u, w, 0, at_z(steps[dr] * k), pb)
        dst = rbs[u][w].at[pb, 0, dr, min(k, FAR - 1)]
        if k >= reach_r and k < far_of(dr, pb):
            rs_copy(u, w, pb, 0, dr, k + 1, True).wait_recv()
            x = x + dst[...].astype(F32)
        elif k > reach_r:
            dst = sb.at[u, w, pb, 0, dr]
        dst[...] = x.astype(BF)
        if k > reach_r:
            rs_copy(u, w, pb, 0, dr, k).start()
        else:
            ry_copy(u, w, pb, dr, k).start()

    def ev_sum_prev0(u, w, pb):
        x = term(u, w, 0, z, pb)
        if reach_r == 0:
            for dr in range(2):
                rs_copy(u, w, pb, 0, dr, 1, True).wait_recv()
                x = x + rbs[u][w][pb, 0, dr, 0].astype(F32)
        rbs[u][w][pb, 0, 0, 0] = x.astype(BF)
        ry_copy(u, w, pb, 0, 0).start()

    def f_copy(u, w):
        return copy(f_s.at[u, w], f_r.at[u, w], f_sem, (u, w), dev(flip=True))

    def ev_sum_home(u, w, pb):
        x = term(u, w, 1, z, pb)
        for dr in range(2):
            rs_copy(u, w, pb, 1, dr, 1, True).wait_recv()
            x = x + rbs[u][w][pb, 1, dr, 0].astype(F32)
        ry_copy(u, w, pb, 0, 0).wait_recv()
        x = x + yb[u, w, pb, 2].astype(F32)
        if pb == 0:
            finish(u, w, c, x)
        else:
            f_s[u, w] = x
            start(f_copy(u, w))

    def ev_finish(u, w, pb):
        if pb == 1:
            f_copy(u, w).wait_recv()
            finish(u, w, other, f_r[u, w])

    def finish(u, w, core, x):
        at = cols((core * 2 + u) * D)
        x = x.T
        if w == 0:
            x = rot(x * (1.0 / LOG2E), cos_own, -sin_own)
            kgr_ref[:, at] = x.astype(BF)
        else:
            vgr_ref[:, at] = x.astype(BF)

    for u in range(2):
        for w in range(2):
            start(kv_chip(u, w, 0))
    events = (
        (ev_begin, 3),
        (ev_own, 5),
        (ev_prev, 5),
        (ev_prev0, 3),
        (ev_sum_own, 5),
        (ev_sum_prev, 5),
        (ev_sum_prev0, 3),
        (ev_sum_home, 3),
        (ev_finish, 3),
        (scores, 3),
        (attend, 3),
        (back, 3),
        (key_grads, 2),
        (value_grads, 2),
        (q_rope, 1),
        (do_send, 1),
        (setup, 0),
    )
    for item in ORDER:
        run, count = events[item // 100000]
        run(*[item // 10 ** (4 - i) % 10 for i in range(count)])
    for u in range(2):
        for which in range(2):
            o_copy(u, which, other).wait_recv()
    for d in sends:
        d.wait_send()
    for kind in range(2):
        for u in range(2):
            for w in range(2):
                assert len(places[kind, u, w]) == PIECES
                every = kvs[u][w].at[pl.ds(0, PIECES)]
                pltpu.make_async_remote_copy(
                    src_ref=every,
                    dst_ref=every,
                    send_sem=ring_sem.at[kind, u, w],
                    recv_sem=ag_sem.at[0, 0, 0],
                    device_id=dev(dz=1),
                    device_id_type=MESH,
                ).wait_send()


def scratch_groups(tok, n_blocks):
    V = pltpu.VMEM
    dma = pltpu.SemaphoreType.DMA
    sems = [dma((8,)), dma((2, 2, 2)), dma((2, 2, PIECES)), dma((2, 2, PIECES))]
    sems += [dma((2, 2))] * 8
    return [
        [V((2 * GB, BLK, D), BF)] * 4,
        [V((2, KB + 1, D, BLK), BF)] * 4,
        [V((2, 2, 2, FAR, D, BLK), BF)] * 4,
        [V((2, 2, BLK, D), BF)] + [V((tok, HALF), BF)] * 6,
        [
            V((2, 2, 2, 2, 2, D, BLK), BF),
            V((2, 2, 2, 5, D, BLK), BF),
            V((2, 2, D, BLK), F32),
            V((2, 2, D, BLK), F32),
        ],
        [
            pltpu.SMEM((KB, n_blocks), jnp.int32),
            pltpu.SMEM((n_blocks,), jnp.int32),
            pltpu.SMEM((n_blocks,), jnp.int32),
            V((1, D), F32),
            V((tok, HEADS * D), BF),
            V((tok, KV_HEADS * D), BF),
            V((tok, KV_HEADS * D), BF),
            V((tok, HEADS * D), BF),
            V((2, BLK, D), F32),
            V((2, BLK, D), F32),
        ],
        [
            V((2, NK, D), BF),
            V((2, NK, 2 * D), BF),
            V((ROWS, NK), F32),
            V((2, 8 * BLK, NK), BF),
            V((2, 8 * BLK, NK), BF),
            V((2, D, 8 * BLK), BF),
            V((2, D, 8 * BLK), BF),
            V((2, 8 * BLK, D), BF),
            V((2, 8 * BLK, D), F32),
            pltpu.SMEM((2, 2 * GB), jnp.int32),
        ],
        sems,
    ]


def split(refs):
    out, at = [], 0
    for n in [8, 4] + [len(x) for x in scratch_groups(BLK, 2 * GB)]:
        out.append(refs[at : at + n])
        at += n
    return out


def store(*refs):
    copies = [pltpu.make_async_copy(refs[i], refs[4 + i], refs[8].at[i]) for i in range(4)]
    for d in copies:
        d.start()
    for d in copies:
        d.wait()


def local(n_grp, n_seq, q, k, v, do, key_blocks, key_counts, block_position):
    vm = pl.BlockSpec(memory_space=pltpu.VMEM)
    hbm = pl.BlockSpec(memory_space=pltpu.HBM)
    scratch = [x for group in scratch_groups(q.shape[0], key_counts.shape[0]) for x in group]
    shapes = [jax.ShapeDtypeStruct(x.shape, BF) for x in (q, q, k, k)]
    operands = [
        pltpu.with_memory_space_constraint(x, pltpu.HBM)
        for x in (key_blocks.T, key_counts, block_position, jnp.asarray(FREQ), q, k, v, do)
    ]
    results = pl.pallas_call(
        functools.partial(kernel, n_grp, n_seq // 2, REACH, REACH_R),
        out_shape=shapes,
        in_specs=[hbm] * 8,
        out_specs=[vm] * 4,
        scratch_shapes=scratch,
        compiler_params=pltpu.CompilerParams(
            collective_id=0, has_side_effects=True, vmem_limit_bytes=48 * 2**20
        ),
    )(*operands)
    return pl.pallas_call(
        store,
        out_shape=shapes,
        in_specs=[pl.BlockSpec(memory_space=pl.ANY)] * 4,
        out_specs=[hbm] * 4,
        scratch_shapes=[pltpu.SemaphoreType.DMA((4,))],
        compiler_params=pltpu.CompilerParams(vmem_limit_bytes=2**20),
    )(*results)


def solution(mesh):
    rows = P(("grp", "seq"), None)
    return jax.shard_map(
        functools.partial(local, mesh.shape["grp"], mesh.shape["seq"]),
        mesh=mesh,
        in_specs=(rows, rows, rows, rows, P(), P(), P()),
        out_specs=(rows, rows, rows, rows),
        check_vma=False,
    )
```

time: 459 us -> 95.2 us (0.21)
  waiting for transfers between devices: 164 us -> 0 us
  other arithmetic: 98.2 us -> 0 us
  Pallas kernels: 0 us -> 94.2 us
  matrix products: 90.5 us -> 0 us
  local copies, waits for them, and re-layouts: 58.1 us -> 0 us
  starting transfers between devices: 41.7 us -> 0 us
    all_to_all x6 -> x0, waiting for transfers between devices: 118 us -> none  [the longest x1 44.3 us: local(): lax.all_to_all(summed, 'seq', split_axis=0, concat_axis=1, tiled=True)]
    pallas_call x0 -> x2, Pallas kernels: none -> 94.2 us  [the longest x1 92.8 us: local(): pl.pallas_call(functools.partial(kernel, n_grp, n_seq // 2, REACH, REACH_...]
    dot_general x24 -> x0, matrix products: 90.5 us -> none  [the longest x4 22.4 us: advance(): jnp.einsum('strd,sjud->srtju', grad_here, value_here, preferred_element_t...]
    scatter-add x8 -> x0, other arithmetic: 80.4 us -> none  [the longest x4 41.6 us: advance(): key_acc = key_acc.at[flat_list].add(key_part.reshape(-1, BLK, HEAD_DIM))]
    ppermute x2 -> x0, waiting for transfers between devices: 45.3 us -> none  [from_behind(): return lax.ppermute(array, axis, pairs)]
    all_to_all x6 -> x0, starting transfers between devices: 36.2 us -> none  [the longest x1 9.97 us: local(): lax.all_to_all(spread, 'seq', split_axis=1, concat_axis=0, tiled=True)]
    gather x8 -> x0, local copies, waits for them, and re-layouts: 17.6 us -> none  [the longest x4 8.99 us: advance(): key_here = key_table[listed_here]]
    unnamed x29 -> x0, local copies, waits for them, and re-layouts: 11.5 us -> none
  transfers between devices with their start and end apart: 8 -> 0, of which waited for: 6 -> 0; matrix products, arithmetic and copies ran while one was open for 5% -> 0% of each run, Pallas kernels for 0% -> 0%
where the time goes in v2:
time: 95.2 us; the launch traced here: 95.1 us
  Pallas kernels  94.2 us (99%)
    pallas_call x1, Pallas kernels, local(): pl.pallas_call(functools.partial(kernel, n_grp, n_seq // 2, REACH, REACH_...  92.8 us

profile of v2, /device:TPU:1, one launch (start us, length us, event | category | flops | bytes accessed | tf_op | source)
XLA Modules:
  0.0 95.1 jit_solution(17209915912338464104)
XLA Ops:
  0.6 92.8 %shard_map.111 = (bf16[128,4096]{1,0:T(8,128)(2,1)S(1)}, bf16[128,4096]{1,0:T(8,128)(2,1)S(1)}, bf16[128,512]{1,0:T(8,128)(2,1)S(1)}, bf16[128,512]{1,0:T(8,128)(2,1)S(1)}) custom-call(s32[12,256]{1,0:T(8,128)} %bitcast.1, s32[256]{0:T(256)} %refs_1_.1, s32[256]{0:T(256)} %refs_2_.1, f32[1,128]{1,0:T(1,128)} %constant.2.clone.refs_3_, ...), custom_call_target="tpu_custom_call" | custom-call | tf_op jit(solution)/shard_map/pallas_call | solution.py:585
  93.4 1.4 %shard_map.112 = (bf16[128,4096]{1,0:T(8,128)(2,1)}, bf16[128,4096]{1,0:T(8,128)(2,1)}, bf16[128,512]{1,0:T(8,128)(2,1)}, bf16[128,512]{1,0:T(8,128)(2,1)}) custom-call(bf16[128,4096]{1,0:T(8,128)(2,1)S(1)} %get-tuple-element.8.refs_0_, bf16[128,4096]{1,0:T(8,128)(2,1)S(1)} %get-tuple-element.9.refs_1_, bf16[128,512]{1,0:T(8,128)(2,1)S(1)} %get-tuple-element.10.refs_2_, ...), custom_call_target="tpu_custom_call" | custom-call | tf_op jit(solution)/shard_map/pallas_call | solution.py:595

commit v3 on v2

--- a/solution.py
+++ b/solution.py
@@ -28,36 +28,38 @@
 PIECES = 30
 FREQ = np.tile(500000.0 ** (-np.arange(D // 2) / (D // 2)), 2).astype(np.float32)[None]
 FAR = 4
-REACH = 2
-REACH_R = 2
+REACH = (2, 3)
+REACH_R = (2, 2)
+MAX_REACH = 3
 ORDER = (
-    0, 1500000, 1400000, 100, 1600000, 1410000, 1510000, 1000, 300000, 100001, 100011, 300100,
-    100101, 100111, 1100, 301000, 101001, 101011, 200001, 100002, 100012, 200011, 100102, 100112,
-    200101, 101101, 101111, 200111, 101002, 101012, 301100, 100003, 100013, 201001, 201011,
-    100103, 100113, 200002, 101102, 101112, 200012, 101003, 101013, 200102, 10000, 100004, 200112,
-    201101, 100114, 200003, 201111, 101113, 101103, 201002, 10100, 200013, 101004, 201012, 110011,
-    200103, 201102, 200113, 110001, 201112, 11000, 200004, 101114, 310000, 201003, 110111, 310100,
-    110101, 201013, 210011, 11100, 201103, 110012, 210001, 110002, 200114, 901000, 201113, 311000,
-    111001, 901100, 201004, 210101, 210111, 110102, 111011, 900000, 110112, 311100, 111101,
-    111111, 900100, 210012, 210002, 110003, 110013, 201114, 1001000, 211001, 111002, 1001100,
-    210102, 110103, 111012, 1000000, 110113, 211011, 111102, 1000100, 210112, 111112, 1301000,
-    210003, 210013, 211101, 1300000, 110004, 501001, 501004, 501011, 501013, 501101, 501103,
-    501111, 501114, 401004, 401013, 401103, 401114, 601000, 601100, 211002, 211111, 111003,
-    111013, 1101000, 210103, 110114, 211012, 210113, 211102, 111103, 1101100, 210004, 211112,
-    111113, 1100000, 501003, 501012, 501102, 501113, 1100100, 401003, 401113, 1201000, 211003,
-    211013, 1200000, 210114, 111004, 500001, 500004, 500011, 500013, 500101, 211103, 500103,
-    211113, 500111, 500114, 400004, 400013, 400103, 400114, 600000, 401012, 600100, 911000,
-    501002, 501112, 401102, 111114, 911100, 211004, 910000, 500003, 500012, 910100, 211114,
-    500102, 1011000, 500113, 400003, 1011100, 401101, 400113, 1010000, 401011, 500002, 1010100,
-    401002, 1311000, 401112, 1310000, 500112, 400012, 511001, 511004, 511011, 511013, 400102,
-    511101, 511103, 511111, 511114, 411004, 411013, 411103, 411114, 611000, 611100, 1111000,
-    400002, 401001, 1111100, 401111, 1110000, 400011, 400101, 400112, 511003, 511012, 511113,
-    1110100, 511102, 411003, 1211000, 411113, 701100, 400001, 1210000, 701000, 510001, 510004,
-    510011, 510013, 510101, 510103, 510111, 510114, 410004, 410013, 410103, 411012, 410114,
-    610000, 610100, 400111, 511002, 511112, 411102, 801100, 700000, 801000, 510003, 510012,
-    510102, 510113, 410003, 800000, 411011, 411101, 410113, 510002, 700100, 411002, 510112,
-    411112, 410012, 410102, 800100, 410002, 411001, 410112, 411111, 410011, 410101, 410001,
-    711000, 410111, 711100, 710000, 811000, 710100, 811100, 810000, 810100,
+    0, 1000, 100, 1100, 1600000, 1500000, 100001, 100011, 1400000, 101001, 300000, 100111, 101111,
+    101011, 100101, 100012, 100002, 1410000, 100112, 101002, 101112, 101101, 101012, 100102,
+    10100, 10000, 1700000, 100013, 200012, 100003, 300100, 101113, 200002, 200101, 101102,
+    1800000, 101003, 301100, 200112, 100103, 100113, 110001, 201001, 201002, 110011, 201112,
+    200003, 201012, 100004, 200113, 101103, 1510000, 200102, 110111, 200001, 11100, 11000, 201003,
+    110012, 200111, 201101, 110002, 101114, 310100, 201102, 200013, 201111, 100114, 201013,
+    200011, 200004, 201011, 301000, 310000, 101013, 110101, 201113, 210001, 101004, 200114,
+    200103, 901000, 900000, 110112, 111001, 900100, 111111, 111011, 901100, 311100, 201004,
+    201114, 110003, 201103, 1000000, 1001000, 110113, 110102, 1000100, 111002, 1001100, 111112,
+    111101, 210012, 1300000, 110013, 1301000, 501114, 401004, 501013, 501004, 1101000, 601100,
+    211011, 401114, 110103, 210003, 501103, 111003, 1100000, 210113, 111102, 1101100, 501113,
+    501003, 111113, 111012, 210011, 501101, 601000, 1100100, 110004, 210111, 401003, 501012,
+    501102, 211001, 401013, 1200000, 401103, 110114, 210112, 1201000, 800000, 311000, 210114,
+    210013, 210004, 401113, 210002, 500004, 500011, 210103, 211101, 210102, 210101, 211111,
+    211002, 111004, 501112, 500001, 501011, 500013, 500111, 400004, 600000, 111103, 910000,
+    211003, 500103, 501002, 500101, 111013, 211102, 501111, 600100, 211113, 911000, 401102,
+    501001, 911100, 400114, 400103, 801000, 401012, 211103, 910100, 500114, 211112, 111114,
+    401112, 211013, 500003, 211012, 211114, 211004, 1011000, 400013, 500012, 1010000, 1011100,
+    401101, 1010100, 400113, 500102, 1310000, 500002, 500113, 1311000, 511114, 411004, 411114,
+    511013, 511004, 511001, 401002, 411103, 511103, 511111, 1110000, 401111, 1111000, 511101,
+    411013, 401011, 611000, 611100, 400003, 400012, 400102, 1111100, 511113, 500112, 511011,
+    411003, 411113, 1211000, 1110100, 1210000, 510114, 510004, 511012, 511003, 511102, 510013,
+    510103, 410004, 400002, 410114, 511112, 610000, 510101, 400112, 510113, 510003, 510012,
+    411012, 401001, 511002, 510102, 410113, 410103, 411102, 400011, 510112, 410013, 410003,
+    400101, 510002, 811000, 701100, 400001, 411112, 810000, 610100, 410102, 400111, 411002,
+    510111, 410112, 410012, 411011, 510011, 801100, 510001, 411111, 410002, 411101, 410101,
+    700100, 410111, 411001, 700000, 410011, 410001, 711100, 800100, 710100, 701000, 711000,
+    811100, 710000, 810100,
 )
 
 
@@ -187,6 +189,8 @@
                     kvs[u][w][slot(1, z, 0)] = x
                 else:
                     ks[u, w] = x
+    loads[0].wait()
+    loads[1].wait()
     pl.semaphore_wait(barrier, len(peers))
 
     def kv_chip(u, w, pb):
@@ -219,21 +223,21 @@
         ag_copy(u, w, pb, 1, dr, k, True).wait_recv()
         if k < far_of(dr, pb):
             ag_copy(u, w, pb, 1, dr, k + 1, False).start()
-        if k <= reach:
+        if k <= reach[u]:
             ay_copy(u, w, pb, -steps[dr] * k).start()
 
     def ev_prev0(u, w, pb):
         ay_copy(u, w, pb, 0).wait_recv()
-        if reach < 1:
+        if reach[u] < 1:
             for dr in range(2):
                 ag_copy(u, w, pb, 0, dr, 1, False).start()
 
     def ev_prev(u, w, pb, dr, k):
-        if k <= reach:
+        if k <= reach[u]:
             ay_copy(u, w, pb, -steps[dr] * k).wait_recv()
         else:
             ag_copy(u, w, pb, 0, dr, k, True).wait_recv()
-        if reach < k + 1 <= far_of(dr, pb):
+        if reach[u] < k + 1 <= far_of(dr, pb):
             ag_copy(u, w, pb, 0, dr, k + 1, False).start()
 
     def q_rope(u):
@@ -258,16 +262,16 @@
             inv[b, kb] = found
         return carry
 
-    def setup():
-        loads[0].wait()
-        loads[1].wait()
-        tables(0)
+    def invert_all():
         for b in range(2):
-            vg[b, :, D:] = jnp.ones((NK, D), BF)
             for u in range(2):
                 for w in range(2):
                     pts[u][w][b, KB] = jnp.zeros((D, BLK), BF)
         lax.fori_loop(0, 2 * GB, invert, 0)
+
+    def set_ones():
+        for b in range(2):
+            vg[b, :, D:] = jnp.ones((NK, D), BF)
 
     rr = lax.broadcasted_iota(jnp.int32, (ROWS, BLK), 0) & (BLK - 1)
     cc = lax.broadcasted_iota(jnp.int32, (ROWS, BLK), 1)
@@ -400,7 +404,7 @@
     def ry_copy(u, w, pb, dr, k):
         at = k if dr == 0 else -k
         src = rbs[u][w].at[pb, 0, dr, k]
-        return ring_copy(src, yb.at[u, w, pb, at + 2], 1, u, w, (pb, at), dev(dg=-1))
+        return ring_copy(src, yb.at[u, w, pb, at + MAX_REACH], 1, u, w, (pb, at), dev(dg=-1))
 
     def ev_sum_own(u, w, pb, dr, k):
         x = term(u, w, 1, at_z(steps[dr] * k), pb)
@@ -409,29 +413,29 @@
             rs_copy(u, w, pb, 1, dr, k + 1, True).wait_recv()
             dst = rbs[u][w].at[pb, 1, dr, k]
             x = x + dst[...].astype(F32)
-        if k <= reach_r:
+        if k <= reach_r[u]:
             ry_copy(u, w, pb, dr, k).wait_recv()
-            x = x + yb[u, w, pb, (k if dr == 0 else -k) + 2].astype(F32)
+            x = x + yb[u, w, pb, (k if dr == 0 else -k) + MAX_REACH].astype(F32)
         dst[...] = x.astype(BF)
         rs_copy(u, w, pb, 1, dr, k).start()
 
     def ev_sum_prev(u, w, pb, dr, k):
         x = term(u, w, 0, at_z(steps[dr] * k), pb)
         dst = rbs[u][w].at[pb, 0, dr, min(k, FAR - 1)]
-        if k >= reach_r and k < far_of(dr, pb):
+        if k >= reach_r[u] and k < far_of(dr, pb):
             rs_copy(u, w, pb, 0, dr, k + 1, True).wait_recv()
             x = x + dst[...].astype(F32)
-        elif k > reach_r:
+        elif k > reach_r[u]:
             dst = sb.at[u, w, pb, 0, dr]
         dst[...] = x.astype(BF)
-        if k > reach_r:
+        if k > reach_r[u]:
             rs_copy(u, w, pb, 0, dr, k).start()
         else:
             ry_copy(u, w, pb, dr, k).start()
 
     def ev_sum_prev0(u, w, pb):
         x = term(u, w, 0, z, pb)
-        if reach_r == 0:
+        if reach_r[u] == 0:
             for dr in range(2):
                 rs_copy(u, w, pb, 0, dr, 1, True).wait_recv()
                 x = x + rbs[u][w][pb, 0, dr, 0].astype(F32)
@@ -447,7 +451,7 @@
             rs_copy(u, w, pb, 1, dr, 1, True).wait_recv()
             x = x + rbs[u][w][pb, 1, dr, 0].astype(F32)
         ry_copy(u, w, pb, 0, 0).wait_recv()
-        x = x + yb[u, w, pb, 2].astype(F32)
+        x = x + yb[u, w, pb, MAX_REACH].astype(F32)
         if pb == 0:
             finish(u, w, c, x)
         else:
@@ -488,7 +492,9 @@
         (value_grads, 2),
         (q_rope, 1),
         (do_send, 1),
-        (setup, 0),
+        (functools.partial(tables, 0), 0),
+        (invert_all, 0),
+        (set_ones, 0),
     )
     for item in ORDER:
         run, count = events[item // 100000]
@@ -525,7 +531,7 @@
         [V((2, 2, BLK, D), BF)] + [V((tok, HALF), BF)] * 6,
         [
             V((2, 2, 2, 2, 2, D, BLK), BF),
-            V((2, 2, 2, 5, D, BLK), BF),
+            V((2, 2, 2, 2 * MAX_REACH + 1, D, BLK), BF),
             V((2, 2, D, BLK), F32),
             V((2, 2, D, BLK), F32),
         ],

time: 95.2 us -> 88.3 us (0.928)
  Pallas kernels: 94.2 us -> 87.4 us
    pallas_call x1, Pallas kernels: 92.8 us -> 86 us  [local(): pl.pallas_call(functools.partial(kernel, n_grp, n_seq // 2, REACH, REACH_...]
where the time goes in v3:
time: 88.3 us; the launch traced here: 88.2 us
  Pallas kernels  87.4 us (99%)
    pallas_call x1, Pallas kernels, local(): pl.pallas_call(functools.partial(kernel, n_grp, n_seq // 2, REACH, REACH_...  86 us

profile of v3, /device:TPU:1, one launch (start us, length us, event | category | flops | bytes accessed | tf_op | source)
XLA Modules:
  0.0 88.2 jit_solution(16822267227710689433)
XLA Ops:
  0.6 86.0 %shard_map.111 = (bf16[128,4096]{1,0:T(8,128)(2,1)S(1)}, bf16[128,4096]{1,0:T(8,128)(2,1)S(1)}, bf16[128,512]{1,0:T(8,128)(2,1)S(1)}, bf16[128,512]{1,0:T(8,128)(2,1)S(1)}) custom-call(s32[12,256]{1,0:T(8,128)} %bitcast.1, s32[256]{0:T(256)} %refs_1_.1, s32[256]{0:T(256)} %refs_2_.1, f32[1,128]{1,0:T(1,128)} %constant.2.clone.refs_3_, ...), custom_call_target="tpu_custom_call" | custom-call | tf_op jit(solution)/shard_map/pallas_call | solution.py:591
  86.6 1.4 %shard_map.112 = (bf16[128,4096]{1,0:T(8,128)(2,1)}, bf16[128,4096]{1,0:T(8,128)(2,1)}, bf16[128,512]{1,0:T(8,128)(2,1)}, bf16[128,512]{1,0:T(8,128)(2,1)}) custom-call(bf16[128,4096]{1,0:T(8,128)(2,1)S(1)} %get-tuple-element.8.refs_0_, bf16[128,4096]{1,0:T(8,128)(2,1)S(1)} %get-tuple-element.9.refs_1_, bf16[128,512]{1,0:T(8,128)(2,1)S(1)} %get-tuple-element.10.refs_2_, ...), custom_call_target="tpu_custom_call" | custom-call | tf_op jit(solution)/shard_map/pallas_call | solution.py:601

commit v4 on v3

--- a/solution.py
+++ b/solution.py
@@ -32,34 +32,34 @@
 REACH_R = (2, 2)
 MAX_REACH = 3
 ORDER = (
-    0, 1000, 100, 1100, 1600000, 1500000, 100001, 100011, 1400000, 101001, 300000, 100111, 101111,
-    101011, 100101, 100012, 100002, 1410000, 100112, 101002, 101112, 101101, 101012, 100102,
-    10100, 10000, 1700000, 100013, 200012, 100003, 300100, 101113, 200002, 200101, 101102,
-    1800000, 101003, 301100, 200112, 100103, 100113, 110001, 201001, 201002, 110011, 201112,
-    200003, 201012, 100004, 200113, 101103, 1510000, 200102, 110111, 200001, 11100, 11000, 201003,
-    110012, 200111, 201101, 110002, 101114, 310100, 201102, 200013, 201111, 100114, 201013,
-    200011, 200004, 201011, 301000, 310000, 101013, 110101, 201113, 210001, 101004, 200114,
-    200103, 901000, 900000, 110112, 111001, 900100, 111111, 111011, 901100, 311100, 201004,
-    201114, 110003, 201103, 1000000, 1001000, 110113, 110102, 1000100, 111002, 1001100, 111112,
-    111101, 210012, 1300000, 110013, 1301000, 501114, 401004, 501013, 501004, 1101000, 601100,
-    211011, 401114, 110103, 210003, 501103, 111003, 1100000, 210113, 111102, 1101100, 501113,
-    501003, 111113, 111012, 210011, 501101, 601000, 1100100, 110004, 210111, 401003, 501012,
-    501102, 211001, 401013, 1200000, 401103, 110114, 210112, 1201000, 800000, 311000, 210114,
-    210013, 210004, 401113, 210002, 500004, 500011, 210103, 211101, 210102, 210101, 211111,
-    211002, 111004, 501112, 500001, 501011, 500013, 500111, 400004, 600000, 111103, 910000,
-    211003, 500103, 501002, 500101, 111013, 211102, 501111, 600100, 211113, 911000, 401102,
-    501001, 911100, 400114, 400103, 801000, 401012, 211103, 910100, 500114, 211112, 111114,
-    401112, 211013, 500003, 211012, 211114, 211004, 1011000, 400013, 500012, 1010000, 1011100,
-    401101, 1010100, 400113, 500102, 1310000, 500002, 500113, 1311000, 511114, 411004, 411114,
-    511013, 511004, 511001, 401002, 411103, 511103, 511111, 1110000, 401111, 1111000, 511101,
-    411013, 401011, 611000, 611100, 400003, 400012, 400102, 1111100, 511113, 500112, 511011,
-    411003, 411113, 1211000, 1110100, 1210000, 510114, 510004, 511012, 511003, 511102, 510013,
-    510103, 410004, 400002, 410114, 511112, 610000, 510101, 400112, 510113, 510003, 510012,
-    411012, 401001, 511002, 510102, 410113, 410103, 411102, 400011, 510112, 410013, 410003,
-    400101, 510002, 811000, 701100, 400001, 411112, 810000, 610100, 410102, 400111, 411002,
-    510111, 410112, 410012, 411011, 510011, 801100, 510001, 411111, 410002, 411101, 410101,
-    700100, 410111, 411001, 700000, 410011, 410001, 711100, 800100, 710100, 701000, 711000,
-    811100, 710000, 810100,
+    0, 1000, 1400000, 100, 1100, 10100, 1700000, 100001, 101001, 100011, 1800000, 100111, 101111,
+    100101, 1600000, 101011, 200001, 100002, 100112, 101002, 100102, 101112, 1500000, 100012,
+    101101, 101012, 110111, 100003, 10000, 201011, 101003, 200002, 200112, 100113, 101113, 101102,
+    201002, 200011, 1410000, 200102, 110001, 201112, 200012, 200113, 200003, 11000, 201003,
+    100103, 310100, 110112, 301000, 201101, 101013, 11100, 101103, 200013, 210111, 201113, 100013,
+    201012, 200111, 101114, 301100, 100114, 300100, 201111, 200101, 110002, 200103, 100004,
+    300000, 101004, 310000, 201001, 110011, 200004, 201102, 110101, 200114, 900000, 900100,
+    111001, 901000, 110113, 111111, 201004, 901100, 201013, 111011, 201103, 201114, 110003,
+    1000000, 1000100, 111002, 110102, 210011, 1001000, 1001100, 110012, 111101, 111112, 1300000,
+    1301000, 501004, 1101000, 111003, 210003, 501111, 311100, 501114, 501013, 311000, 111012,
+    501103, 211111, 210113, 1101100, 111113, 110103, 210001, 210012, 1201000, 401114, 110013,
+    210101, 210112, 210002, 501003, 111102, 501011, 110004, 1100000, 110114, 501001, 1510000,
+    1100100, 501101, 401004, 501113, 1200000, 210114, 211113, 501102, 501012, 211003, 500103,
+    210102, 500011, 500004, 801000, 211011, 210004, 210103, 500001, 211002, 400103, 500013,
+    601000, 211112, 210013, 211001, 111103, 401103, 111013, 500111, 400114, 401013, 500114,
+    911000, 400004, 910000, 910100, 211012, 401003, 211102, 211114, 911100, 501002, 500102,
+    801100, 501112, 400013, 211101, 401113, 211013, 211004, 500012, 211103, 111004, 111114,
+    1011000, 1010000, 601100, 600000, 1011100, 500003, 401102, 500101, 1010100, 500113, 1311000,
+    401012, 1310000, 511004, 511013, 401002, 511103, 411103, 511114, 1111000, 611100, 400113,
+    600100, 411013, 1111100, 411004, 400012, 511101, 411114, 400003, 511011, 1110000, 500112,
+    511012, 511113, 401101, 401001, 401011, 401112, 511003, 1110100, 511001, 1211000, 511111,
+    400102, 400011, 1210000, 510004, 510114, 511102, 410114, 410004, 510013, 810000, 510103,
+    510101, 511002, 610100, 811100, 410013, 500002, 511112, 411003, 510003, 800100, 510113,
+    810100, 701000, 410103, 411102, 410003, 411113, 410113, 411012, 510012, 411002, 510102,
+    510002, 400112, 510112, 400002, 401111, 510001, 510011, 800000, 510111, 411112, 411101,
+    410012, 410102, 411011, 410002, 411001, 400101, 811000, 410112, 400111, 411111, 400001,
+    410011, 611000, 410001, 610000, 410101, 410111, 711100, 700100, 701100, 710000, 700000,
+    711000, 710100,
 )
 
 
@@ -109,12 +109,19 @@
     blk = (c, other)
     steps = (1, -1)
 
+    turns, devices = {}, {}
+
     def at_z(off):
-        return lax.rem(z + off + 2 * n_z, n_z)
+        if off not in turns:
+            turns[off] = lax.rem(z + (off + 2 * n_z), n_z)
+        return turns[off]
 
     def dev(dg=0, dz=0, flip=False):
-        core = other if flip else c
-        return {"grp": lax.rem(g + dg + n_grp, n_grp), "seq": at_z(dz) * 2 + core}
+        at = (dg, dz, flip)
+        if at not in devices:
+            core = other if flip else c
+            devices[at] = {"grp": lax.rem(g + (dg + n_grp), n_grp), "seq": at_z(dz) * 2 + core}
+        return devices[at]
 
     sends = []
 
@@ -147,7 +154,10 @@
         )
 
     barrier = pltpu.get_barrier_semaphore()
-    peers = [dev(flip=True), dev(dz=1), dev(dz=-1), dev(dg=1), dev(dg=-1)]
+    peers = [dev(flip=True)]
+    for flip in (False, True):
+        peers += [dev(dz=1, flip=flip), dev(dz=-1, flip=flip)]
+        peers += [dev(dg=1, flip=flip), dev(dg=-1, flip=flip)]
     for p in peers:
         pl.semaphore_signal(barrier, inc=1, device_id=p, device_id_type=MESH)
 
@@ -399,12 +409,14 @@
         else:
             src = rbs[u][w].at[pb, grp, dr, min(k, FAR - 1)]
         dst = rbs[u][w].at[pb, grp, dr, k - 1]
-        return ring_copy(src, dst, 1, u, w, (pb, grp, dr, k), dev(dz=steps[dr]))
+        to = dev(dz=steps[dr], flip=grp == 1 and pb == 1 and k == 1)
+        return ring_copy(src, dst, 1, u, w, (pb, grp, dr, k), to)
 
     def ry_copy(u, w, pb, dr, k):
         at = k if dr == 0 else -k
         src = rbs[u][w].at[pb, 0, dr, k]
-        return ring_copy(src, yb.at[u, w, pb, at + MAX_REACH], 1, u, w, (pb, at), dev(dg=-1))
+        to = dev(dg=-1, flip=pb == 1 and k == 0)
+        return ring_copy(src, yb.at[u, w, pb, at + MAX_REACH], 1, u, w, (pb, at), to)
 
     def ev_sum_own(u, w, pb, dr, k):
         x = term(u, w, 1, at_z(steps[dr] * k), pb)
@@ -446,22 +458,22 @@
         return copy(f_s.at[u, w], f_r.at[u, w], f_sem, (u, w), dev(flip=True))
 
     def ev_sum_home(u, w, pb):
-        x = term(u, w, 1, z, pb)
+        if pb == 0:
+            x = term(u, w, 1, z, 0)
+        else:
+            f_copy(u, w).wait_recv()
+            x = f_r[u, w]
         for dr in range(2):
             rs_copy(u, w, pb, 1, dr, 1, True).wait_recv()
             x = x + rbs[u][w][pb, 1, dr, 0].astype(F32)
         ry_copy(u, w, pb, 0, 0).wait_recv()
         x = x + yb[u, w, pb, MAX_REACH].astype(F32)
-        if pb == 0:
-            finish(u, w, c, x)
-        else:
-            f_s[u, w] = x
+        finish(u, w, blk[pb], x)
+
+    def ev_hand_over(u, w, pb):
+        if pb == 1:
+            f_s[u, w] = term(u, w, 1, z, 1)
             start(f_copy(u, w))
-
-    def ev_finish(u, w, pb):
-        if pb == 1:
-            f_copy(u, w).wait_recv()
-            finish(u, w, other, f_r[u, w])
 
     def finish(u, w, core, x):
         at = cols((core * 2 + u) * D)
@@ -484,7 +496,7 @@
         (ev_sum_prev, 5),
         (ev_sum_prev0, 3),
         (ev_sum_home, 3),
-        (ev_finish, 3),
+        (ev_hand_over, 3),
         (scores, 3),
         (attend, 3),
         (back, 3),

time: 88.3 us -> 86.6 us (0.981)
  Pallas kernels: 87.4 us -> 85.7 us
    pallas_call x1, Pallas kernels: 86 us -> 84.3 us  [local(): pl.pallas_call(functools.partial(kernel, n_grp, n_seq // 2, REACH, REACH_...]
where the time goes in v4:
time: 86.6 us; the launch traced here: 86.5 us
  Pallas kernels  85.7 us (99%)
    pallas_call x1, Pallas kernels, local(): pl.pallas_call(functools.partial(kernel, n_grp, n_seq // 2, REACH, REACH_...  84.3 us

profile of v4, /device:TPU:1, one launch (start us, length us, event | category | flops | bytes accessed | tf_op | source)
XLA Modules:
  0.0 86.5 jit_solution(6136098499232320529)
XLA Ops:
  0.6 84.3 %shard_map.111 = (bf16[128,4096]{1,0:T(8,128)(2,1)S(1)}, bf16[128,4096]{1,0:T(8,128)(2,1)S(1)}, bf16[128,512]{1,0:T(8,128)(2,1)S(1)}, bf16[128,512]{1,0:T(8,128)(2,1)S(1)}) custom-call(s32[12,256]{1,0:T(8,128)} %bitcast.1, s32[256]{0:T(256)} %refs_1_.1, s32[256]{0:T(256)} %refs_2_.1, f32[1,128]{1,0:T(1,128)} %constant.2.clone.refs_3_, ...), custom_call_target="tpu_custom_call" | custom-call | tf_op jit(solution)/shard_map/pallas_call | solution.py:603
  84.9 1.4 %shard_map.112 = (bf16[128,4096]{1,0:T(8,128)(2,1)}, bf16[128,4096]{1,0:T(8,128)(2,1)}, bf16[128,512]{1,0:T(8,128)(2,1)}, bf16[128,512]{1,0:T(8,128)(2,1)}) custom-call(bf16[128,4096]{1,0:T(8,128)(2,1)S(1)} %get-tuple-element.8.refs_0_, bf16[128,4096]{1,0:T(8,128)(2,1)S(1)} %get-tuple-element.9.refs_1_, bf16[128,512]{1,0:T(8,128)(2,1)S(1)} %get-tuple-element.10.refs_2_, ...), custom_call_target="tpu_custom_call" | custom-call | tf_op jit(solution)/shard_map/pallas_call | solution.py:613
